TPU v7x, 128 devices: a whole 4x4x4 slice. The times are simulated.
128 devices in a mesh: st: 32 (over z, x, core), sb: 4 (over y).
Axes of the slice: x: 4, y: 4, z: 4, core: 2. Of those that a mesh axis runs over, the one named last changes fastest.
Arguments:
- volts: bfloat16 [2, 1024, 126976], P(None, 'st'), may hold values from -6 to 6
- prototype: float32 [16, 4096], replicated, may hold values from -1.5 to 1.5
- beam_channels: int32 [384], replicated, may hold values from 0 to 4095, as said below
- station_index: int32 [256], replicated, may hold values from 0 to 511, as said below
- delays: float32 [256, 256], replicated, may hold values from -64 to 64
- gains: float32 [256, 256], replicated, may hold values from 0.5 to 2
- assign: int32 [384, 1], replicated, may hold values from 0 to 3; in each aligned block of 384 rows (0 to 383, 384 to 767, ...) at most 160 rows name the same one
Outputs:
- visibility: float32 [2, 4, 32, 1024, 1024], P(None, 'sb', 'st')
- beam_out: float32 [4, 160, 2, 16, 512], P('sb', 'st')
Inputs may be any that keep to these rules, and one draw needn't show every extreme that they name: `beam_channels`: 384 different channels. `station_index`: 256 different stations. `assign`: no index of sb receives more than 160 list entries, and some index receives exactly 160; every index receives at least one.
All inputs are finite; a program needn't handle non-finite values.
Results may differ from a plain program's by a relative error of at most 0.0054.
Values may be sent and summed in bfloat16 or wider, within the bound.
A program may use at most 192 MiB of HBM per device.

v0:
```python
import math

import jax
import jax.numpy as jnp
from jax import lax
from jax.sharding import PartitionSpec as P

NCH = 4096
FRAMES = 16
SLOTS = 160


TWO_PI = 2.0 * math.pi


def polyphase(volts, prototype, frame_count):
    tap_count = prototype.shape[0]
    length = prototype.shape[1]
    segments = volts.reshape(2, volts.shape[1], frame_count + tap_count - 1, length)
    summed = jnp.zeros((2, volts.shape[1], frame_count, length), jnp.float32)
    for tap_idx in range(tap_count):
        summed = summed + prototype[tap_idx] * segments[
            :, :, tap_idx : tap_idx + frame_count, :
        ].astype(jnp.float32)
    return summed.astype(jnp.bfloat16)


def dft_tables(channels, length):
    sample_ids = jnp.arange(length, dtype=jnp.int32)
    phase_ids = sample_ids[:, None] * channels[None, :] % length
    angles = phase_ids.astype(jnp.float32) * (TWO_PI / length)
    scale_dft = 1.0 / math.sqrt(length)
    return (
        (jnp.cos(angles) * scale_dft).astype(jnp.bfloat16),
        (jnp.sin(angles) * scale_dft).astype(jnp.bfloat16),
    )


def transform(flat_rows, cos_t, sin_t):
    real_part = jnp.dot(flat_rows[0], cos_t, preferred_element_type=jnp.float32) + jnp.dot(
        flat_rows[1], sin_t, preferred_element_type=jnp.float32
    )
    imag_part = jnp.dot(flat_rows[1], cos_t, preferred_element_type=jnp.float32) - jnp.dot(
        flat_rows[0], sin_t, preferred_element_type=jnp.float32
    )
    return jnp.stack([real_part, imag_part]).astype(jnp.bfloat16)


def correlate(grouped):
    stacked = jnp.concatenate([grouped[0], grouped[1]], axis=1)
    turned = jnp.concatenate([grouped[1], -grouped[0]], axis=1)
    inverse = 1.0 / grouped.shape[2]
    vis_re = jnp.dot(stacked, stacked.T, preferred_element_type=jnp.float32) * inverse
    vis_im = jnp.dot(turned, stacked.T, preferred_element_type=jnp.float32) * inverse
    return jnp.stack([vis_re, vis_im])


def beam_weights(delays, gains, channel, length, listed):
    angles = delays * (channel.astype(jnp.float32) * (TWO_PI / length))
    scaling = gains * (1.0 / math.sqrt(listed))
    return (
        (scaling * jnp.cos(angles)).astype(jnp.bfloat16),
        (-scaling * jnp.sin(angles)).astype(jnp.bfloat16),
    )


def combine(spectrum, w_re, w_im):
    real_in = spectrum[:, 0]
    imag_in = spectrum[:, 1]

    def product(operand, weight):
        return jnp.einsum("sfjp,sbj->sfpb", operand, weight, preferred_element_type=jnp.float32)

    out_re = product(real_in, w_re) - product(imag_in, w_im)
    out_im = product(imag_in, w_re) + product(real_in, w_im)
    stacked = jnp.stack([out_re, out_im], axis=1)
    return stacked.reshape(stacked.shape[0], 2, stacked.shape[2], -1)


def body(volts, prototype, beam_channels, station_index, delays, gains, assign):
    sig_dev = volts.shape[1]
    st_count = lax.axis_size("st")
    sb_count = lax.axis_size("sb")
    sb_here = lax.axis_index("sb")
    st_here = lax.axis_index("st")
    filtered = polyphase(volts, prototype, FRAMES)
    flat_rows = filtered.reshape(2, sig_dev * FRAMES, NCH)
    band_width = NCH // sb_count
    channels = sb_here * band_width + jnp.arange(band_width, dtype=jnp.int32)
    cos_t, sin_t = dft_tables(channels, NCH)
    spectra = transform(flat_rows, cos_t, sin_t).reshape(2, sig_dev, FRAMES, band_width)
    turned_over = lax.all_to_all(spectra, "st", split_axis=3, concat_axis=1, tiled=True)
    signals = turned_over.shape[1]
    visibility = correlate(turned_over.reshape(2, signals, -1)).reshape(2, 1, 1, signals, signals)
    owners = assign[:, 0]
    matches = (owners == sb_here).astype(jnp.int32)
    position = jnp.cumsum(matches) - 1
    slot_ids = jnp.arange(SLOTS, dtype=jnp.int32)
    picker = matches[None, :] * (position[None, :] == slot_ids[:, None]).astype(jnp.int32)
    filled = jnp.sum(picker, axis=1)
    slot_channel = jnp.sum(picker * beam_channels[None, :], axis=1)
    per_dev = SLOTS // st_count
    listed = station_index.shape[0]
    cos_b, sin_b = dft_tables(slot_channel, NCH)
    slot_spectra = transform(flat_rows, cos_b, sin_b) * filled.astype(jnp.bfloat16)[None, None, :]
    slot_spectra = slot_spectra.reshape(2, sig_dev, FRAMES, SLOTS).transpose(3, 0, 2, 1)
    stations_dev = sig_dev // 2
    local_ids = st_here * stations_dev + jnp.arange(stations_dev, dtype=jnp.int32)
    chooser = (station_index[:, None] == local_ids[None, :]).astype(jnp.float32)
    delay_local = jnp.sum(delays[:, :, None] * chooser[None, :, :], axis=1)
    gain_local = jnp.sum(gains[:, :, None] * chooser[None, :, :], axis=1)
    spectrum = slot_spectra.reshape(per_dev * lax.axis_size("st"), 2, FRAMES, stations_dev, 2)
    w_re, w_im = beam_weights(
        delay_local[None], gain_local[None], slot_channel[:, None, None], NCH, listed
    )
    beam_out = lax.psum_scatter(
        combine(spectrum, w_re, w_im), "st", scatter_dimension=0, tiled=True
    )
    beam_out = beam_out.reshape(1, per_dev, 2, FRAMES, -1)
    return (visibility, beam_out)


def solution(mesh):
    in_specs = (P(None, "st", None), P(), P(), P(), P(), P(), P())
    out_specs = (P(None, "sb", "st", None, None), P("sb", "st", None, None, None))
    return jax.shard_map(body, mesh=mesh, in_specs=in_specs, out_specs=out_specs, check_vma=False)
```

profile of v0, /device:TPU:1, one launch (start us, length us, event | category | flops | bytes accessed | tf_op | source)
XLA Modules:
  0.0 638.6 jit_solution(6633204261095407268)
XLA Ops:
  14.8 17.4 %reshape.159 = bf16[2,32,31,4096]{3,2,1,0:T(8,128)(2,1)} reshape(bf16[2,32,126976]{2,1,0:T(8,128)(2,1)} %param.7) | data formatting | bytes 32505856 | tf_op jit(solution)/shard_map/reshape | solution.py:19
  32.2 77.7 %add_convert_fusion = bf16[2,32,16,4096]{3,2,1,0:T(8,128)(2,1)} fusion(bf16[2,32,31,4096]{3,2,1,0:T(8,128)(2,1)} %reshape.159, f32[4096]{0:T(1024)S(1)} %bitcast.115, f32[4096]{0:T(1024)S(1)} %bitcast.116, f32[4096]{0:T(1024)S(1)} %bitcast.102, f32[4096]{0:T(1024)S(1)} %bitcast.103, f32[4096]{0:T(1024)S(1)} %bitcast.104, f32[4096]{0:T(1024)S(1)} %bitcast.105, ...), kind=kLoop, calls=%fused_computation.10 | loop fusion | flops 201326592 | bytes 142868480 | tf_op jit(solution)/shard_map/convert_element_type | solution.py:25
  114.1 9.9 %fusion.47 = f32[512,160]{0,1:T(8,128)S(1)} fusion(bf16[512,4096]{1,0:T(8,128)(2,1)S(1)} %bitcast.88, s32[160]{0:T(256)S(1)} %get-tuple-element.21), kind=kOutput, calls=%fused_computation.67 | convolution fusion | flops 681574400 | bytes 4522624 | tf_op jit(solution)/shard_map/dot_general | solution.py:43
  124.1 10.3 %fusion.48 = f32[512,160]{0,1:T(8,128)S(1)} fusion(bf16[512,4096]{1,0:T(8,128)(2,1)S(1)} %bitcast.92, s32[160]{0:T(256)S(1)} %get-tuple-element.21), kind=kOutput, calls=%fused_computation.68 | convolution fusion | flops 681574400 | bytes 4522624 | tf_op jit(solution)/shard_map/dot_general | solution.py:40
  134.4 10.2 %fusion.53 = bf16[512,160]{0,1:T(8,128)(2,1)S(1)} fusion(f32[512,160]{0,1:T(8,128)S(1)} %fusion.47, bf16[512,4096]{1,0:T(8,128)(2,1)S(1)} %bitcast.93, s32[160]{0:T(256)S(1)} %get-tuple-element.21), kind=kOutput, calls=%fused_computation.73 | convolution fusion | flops 681738240 | bytes 4686464 | tf_op jit(solution)/shard_map/dot_general | solution.py:43
  144.7 12.4 %fusion.54 = bf16[512,160]{0,1:T(8,128)(2,1)S(1)} fusion(f32[512,160]{0,1:T(8,128)S(1)} %fusion.48, bf16[512,4096]{1,0:T(8,128)(2,1)} %bitcast.89, s32[160]{0:T(256)S(1)} %get-tuple-element.21), kind=kOutput, calls=%fused_computation.74 | convolution fusion | flops 681738240 | bytes 4686464 | tf_op jit(solution)/shard_map/dot_general | solution.py:40
  161.2 9.3 %fusion.27 = f32[160,16,2,256]{3,1,2,0:T(8,128)S(1)} fusion(bf16[160,1,16,16,2]{3,2,4,0,1:T(8,128)(2,1)S(1)} %copy.103, f32[160]{0:T(256)S(1)} %convert_multiply_fusion, f32[256,16]{0,1:T(8,128)S(1)} %copy.91, f32[256,16]{0,1:T(8,128)S(1)} %get-tuple-element.47), kind=kOutput, calls=%fused_computation.49 | convolution fusion | flops 43909120 | bytes 5440128 | tf_op jit(solution)/shard_map/sfjp,sbj->sfpb/dot_general | solution.py:72
  170.5 11.5 %fusion.29 = f32[160,16,2,256]{3,1,2,0:T(8,128)} fusion(bf16[160,1,16,16,2]{3,2,4,0,1:T(8,128)(2,1)S(1)} %copy.102, f32[160]{0:T(256)S(1)} %convert_multiply_fusion, f32[256,16]{0,1:T(8,128)S(1)} %copy.91, f32[256,16]{0,1:T(8,128)S(1)} %get-tuple-element.47), kind=kOutput, calls=%fused_computation.50 | convolution fusion | flops 43909120 | bytes 5440128 | tf_op jit(solution)/shard_map/sfjp,sbj->sfpb/dot_general | solution.py:72
  182.0 9.2 %convolution_add_fusion = f32[160,16,2,256]{3,1,2,0:T(8,128)S(1)} fusion(f32[160,16,2,256]{3,1,2,0:T(8,128)S(1)} %fusion.27, bf16[160,1,16,16,2]{3,2,4,0,1:T(8,128)(2,1)S(1)} %copy.102, f32[256,16]{0,1:T(8,128)S(1)} %get-tuple-element.46, f32[160]{0:T(256)S(1)} %convert_multiply_fusion, f32[256,16]{0,1:T(8,128)S(1)} %copy.91), kind=kOutput, calls=%fused_computation.39 | convolution fusion | flops 45219840 | bytes 10683008 | tf_op jit(solution)/shard_map/sfjp,sbj->sfpb/dot_general | solution.py:72
  191.2 7.9 %copy.94 = f32[160,16,2,256]{3,2,1,0:T(2,128)} copy(f32[160,16,2,256]{3,1,2,0:T(8,128)S(1)} %convolution_add_fusion) | data formatting | bytes 10485760 | tf_op jit(solution)/shard_map/add | solution.py:75
  199.1 8.0 %stack.46 = f32[160,1,16,512]{3,2,0,1:T(8,128)} reshape(f32[160,16,2,256]{3,2,1,0:T(2,128)} %copy.94) | data formatting | bytes 10485760 | tf_op jit(solution)/shard_map/stack | solution.py:76
  207.0 12.0 %convolution_subtract_fusion = f32[160,16,2,256]{3,1,2,0:T(8,128)S(1)} fusion(f32[160,16,2,256]{3,1,2,0:T(8,128)} %fusion.29, bf16[160,1,16,16,2]{3,2,4,0,1:T(8,128)(2,1)S(1)} %copy.103, f32[256,16]{0,1:T(8,128)S(1)} %get-tuple-element.46, f32[160]{0:T(256)S(1)} %convert_multiply_fusion, f32[256,16]{0,1:T(8,128)S(1)} %copy.91), kind=kOutput, calls=%fused_computation.40 | convolution fusion | flops 45219840 | bytes 10683008 | tf_op jit(solution)/shard_map/sfjp,sbj->sfpb/dot_general | solution.py:72
  219.1 7.5 %copy.93 = f32[160,16,2,256]{3,2,1,0:T(2,128)} copy(f32[160,16,2,256]{3,1,2,0:T(8,128)S(1)} %convolution_subtract_fusion) | data formatting | bytes 10485760 | tf_op jit(solution)/shard_map/sub | solution.py:74
  226.6 8.0 %stack.45 = f32[160,1,16,512]{3,2,0,1:T(8,128)} reshape(f32[160,16,2,256]{3,2,1,0:T(2,128)} %copy.93) | data formatting | bytes 10485760 | tf_op jit(solution)/shard_map/stack | solution.py:76
  234.5 10.5 %pad_maximum_fusion = f32[160,2,16,512]{3,2,0,1:T(8,128)} fusion(f32[160,1,16,512]{3,2,0,1:T(8,128)} %stack.46, f32[160,1,16,512]{3,2,0,1:T(8,128)} %stack.45), kind=kLoop, calls=%fused_computation.12 | loop fusion | flops 2621440 | bytes 20971520 | tf_op jit(solution)/shard_map/stack | solution.py:76
  245.1 65.7 %fusion.6 = f32[512,1024]{1,0:T(8,128)S(1)} fusion(bf16[512,4096]{1,0:T(8,128)(2,1)} %bitcast.90, s32[1024]{0:T(1024)S(1)} %iota_add_fusion), kind=kOutput, calls=%fused_computation.14 | convolution fusion | flops 4362076160 | bytes 6295552 | tf_op jit(solution)/shard_map/dot_general | solution.py:43
  310.8 63.7 %fusion.7 = f32[512,1024]{1,0:T(8,128)S(1)} fusion(bf16[512,4096]{1,0:T(8,128)(2,1)S(1)} %bitcast.94, s32[1024]{0:T(1024)S(1)} %iota_add_fusion), kind=kOutput, calls=%fused_computation.15 | convolution fusion | flops 4362076160 | bytes 6295552 | tf_op jit(solution)/shard_map/dot_general | solution.py:40
  374.5 63.9 %subtract_convert_fusion = bf16[512,1024]{1,0:T(8,128)(2,1)S(1)} fusion(f32[512,1024]{1,0:T(8,128)S(1)} %fusion.6, bf16[512,4096]{1,0:T(8,128)(2,1)S(1)} %bitcast.95, s32[1024]{0:T(1024)S(1)} %iota_add_fusion), kind=kOutput, calls=%fused_computation.45 | convolution fusion | flops 4363124736 | bytes 7344128 | tf_op jit(solution)/shard_map/dot_general | solution.py:43
  438.4 64.3 %add_convert_fusion.1 = bf16[512,1024]{1,0:T(8,128)(2,1)S(1)} fusion(f32[512,1024]{1,0:T(8,128)S(1)} %fusion.7, bf16[512,4096]{1,0:T(8,128)(2,1)S(1)} %bitcast.91, s32[1024]{0:T(1024)S(1)} %iota_add_fusion), kind=kOutput, calls=%fused_computation.46 | convolution fusion | flops 4363124736 | bytes 7344128 | tf_op jit(solution)/shard_map/dot_general | solution.py:40
  502.9 14.0 %copy.83 = bf16[2,32,16,1024]{1,2,0,3:T(8,128)(2,1)} copy(bf16[2,32,16,1024]{3,2,1,0:T(8,128)(2,1)S(1)} %pad_maximum_fusion.1) | data formatting | bytes 4194304 | tf_op jit(solution)/shard_map/stack | solution.py:46
  516.9 13.3 %reshape.174 = bf16[32,2,16384]{2,1,0:T(2,128)(2,1)} reshape(bf16[1024,2,16,32]{3,2,1,0:T(8,128)(2,1)} %bitcast.85) | data formatting | bytes 4194304
  530.2 9.6 %all-to-all-start = ((bf16[32,2,16384]{2,1,0:T(2,128)(2,1)}), bf16[32,2,16384]{2,1,0:T(2,128)(2,1)S(1)}, u32[]{:S(2)}, u32[]{:S(2)}) async-start(bf16[32,2,16384]{2,1,0:T(2,128)(2,1)} %reshape.174), calls=%async_computation | async-start | bytes 4194304 | tf_op jit(solution)/shard_map/all_to_all | solution.py:92
  541.0 26.6 %all-to-all-done = bf16[32,2,16384]{2,1,0:T(2,128)(2,1)S(1)} async-done(((bf16[32,2,16384]{2,1,0:T(2,128)(2,1)}), bf16[32,2,16384]{2,1,0:T(2,128)(2,1)S(1)}, u32[]{:S(2)}, u32[]{:S(2)}) %all-to-all-start) | async-done | bytes 2097184 | tf_op jit(solution)/shard_map/all_to_all | solution.py:92
  574.0 19.2 %copy.99 = bf16[2,32,16,32,32]{4,3,2,1,0:T(8,128)(2,1)} copy(bf16[2,32,16,32,32]{1,2,0,4,3:T(8,128)(2,1)} %bitcast.86) | data formatting | bytes 4194304 | tf_op jit(solution)/shard_map/all_to_all | solution.py:92
  (52 shorter events, 61.5 us)
Async XLA Ops:
  7.2 622.6 %all-reduce.3.cloned.1.call-start = ((), (), s32[]{:S(2)}) async-start(), calls=%async_computation.1 | async-start | bytes 20971520
  114.1 9.9 %copy-start = (bf16[1,32,16,4096]{3,2,1,0:T(8,128)(2,1)}, bf16[1,32,16,4096]{3,2,1,0:T(8,128)(2,1)S(1)}, u32[]{:S(2)}) copy-start(bf16[1,32,16,4096]{3,2,1,0:T(8,128)(2,1)S(1)} %get-tuple-element.25) | copy-start | bytes 12582916
  114.1 20.3 %copy-start.2 = (bf16[1,32,16,4096]{3,2,1,0:T(8,128)(2,1)}, bf16[1,32,16,4096]{3,2,1,0:T(8,128)(2,1)S(1)}, u32[]{:S(2)}) copy-start(bf16[1,32,16,4096]{3,2,1,0:T(8,128)(2,1)S(1)} %get-tuple-element.24) | copy-start | bytes 12582916
  245.1 65.7 %copy-start.3 = (bf16[1,32,16,4096]{3,2,1,0:T(8,128)(2,1)S(1)}, bf16[1,32,16,4096]{3,2,1,0:T(8,128)(2,1)}, u32[]{:S(2)}) copy-start(bf16[1,32,16,4096]{3,2,1,0:T(8,128)(2,1)} %copy-done.2) | copy-start | bytes 12582916
  374.5 63.9 %copy-start.1 = (bf16[1,32,16,4096]{3,2,1,0:T(8,128)(2,1)S(1)}, bf16[1,32,16,4096]{3,2,1,0:T(8,128)(2,1)}, u32[]{:S(2)}) copy-start(bf16[1,32,16,4096]{3,2,1,0:T(8,128)(2,1)} %copy-done) | copy-start | bytes 12582916
  530.2 9.6 %copy-start.4 = (u32[128]{0:T(128)S(1)}, u32[128]{0:T(128)}, u32[]{:S(2)}) copy-start(u32[128]{0:T(128)} %constant.59) | copy-start | bytes 1540
  530.2 37.4 %all-to-all-start = ((bf16[32,2,16384]{2,1,0:T(2,128)(2,1)}), bf16[32,2,16384]{2,1,0:T(2,128)(2,1)S(1)}, u32[]{:S(2)}, u32[]{:S(2)}) async-start(bf16[32,2,16384]{2,1,0:T(2,128)(2,1)} %reshape.174), calls=%async_computation | async-start | bytes 4194304 | tf_op jit(solution)/shard_map/all_to_all | solution.py:92
Sparse Core Ops, SparseCore 0:
  245.2 129.2 all-reduce.2
where the time goes:
time: 649 us; the launch traced here: 639 us
  matrix products  347 us (53%)
  local copies, waits for them, and re-layouts  142 us (22%)
  other arithmetic  98 us (15%)
  waiting for transfers between devices  26.6 us (4%)
  between operations  15.2 us (2%)
  starting transfers between devices  9.6 us (1%)
    convert_element_type x1, other arithmetic, polyphase(): return summed.astype(jnp.bfloat16)  77.7 us
    dot_general x2, matrix products, transform(): jnp.dot(flat_rows[1], sin_t, preferred_element_type=jnp.float32)  76.7 us
    dot_general x2, matrix products, transform(): jnp.dot(flat_rows[1], cos_t, preferred_element_type=jnp.float32)  75.6 us
    dot_general x2, matrix products, transform(): jnp.dot(flat_rows[0], sin_t, preferred_element_type=jnp.float32)  74.1 us
    dot_general x2, matrix products, transform(): jnp.dot(flat_rows[0], cos_t, preferred_element_type=jnp.float32)  74 us
    dot_general x4, matrix products, product(): jnp.einsum('sfjp,sbj->sfpb', operand, weight, preferred_element_type=jnp....  42 us
    all_to_all x1, waiting for transfers between devices, body(): lax.all_to_all(spectra, 'st', split_axis=3, concat_axis=1, tiled=True)  26.6 us
    unnamed x16, local copies, waits for them, and re-layouts  24.8 us
  transfers between devices with their start and end apart: 2, of which 1 were waited for; matrix products, arithmetic and copies ran while one was open for 54% of the time, Pallas kernels for 0%

commit v1 on v0

--- a/solution.py
+++ b/solution.py
@@ -94,7 +94,9 @@
     visibility = correlate(turned_over.reshape(2, signals, -1)).reshape(2, 1, 1, signals, signals)
     owners = assign[:, 0]
     matches = (owners == sb_here).astype(jnp.int32)
-    position = jnp.cumsum(matches) - 1
+    order = jnp.arange(matches.shape[0], dtype=jnp.int32)
+    earlier = (order[None, :] < order[:, None]).astype(jnp.int32)
+    position = jnp.sum(earlier * matches[None, :], axis=1)
     slot_ids = jnp.arange(SLOTS, dtype=jnp.int32)
     picker = matches[None, :] * (position[None, :] == slot_ids[:, None]).astype(jnp.int32)
     filled = jnp.sum(picker, axis=1)

time: 649 us -> 649 us (level)
  transfers between devices with their start and end apart: 2 -> 2, of which waited for: 1 -> 1; matrix products, arithmetic and copies ran while one was open for 54% -> 55% of each run, Pallas kernels for 0% -> 0%
where the time goes in v1:
time: 649 us; the launch traced here: 638 us
  matrix products  347 us (53%)
  local copies, waits for them, and re-layouts  142 us (22%)
  other arithmetic  97.7 us (15%)
  waiting for transfers between devices  26.6 us (4%)
  between operations  15.4 us (2%)
  starting transfers between devices  9.6 us (1%)
    convert_element_type x1, other arithmetic, polyphase(): return summed.astype(jnp.bfloat16)  77.7 us
    dot_general x2, matrix products, transform(): jnp.dot(flat_rows[1], sin_t, preferred_element_type=jnp.float32)  76.4 us
    dot_general x2, matrix products, transform(): jnp.dot(flat_rows[1], cos_t, preferred_element_type=jnp.float32)  75.9 us
    dot_general x2, matrix products, transform(): jnp.dot(flat_rows[0], sin_t, preferred_element_type=jnp.float32)  74.5 us
    dot_general x2, matrix products, transform(): jnp.dot(flat_rows[0], cos_t, preferred_element_type=jnp.float32)  73.6 us
    dot_general x4, matrix products, product(): jnp.einsum('sfjp,sbj->sfpb', operand, weight, preferred_element_type=jnp....  42 us
    all_to_all x1, waiting for transfers between devices, body(): lax.all_to_all(spectra, 'st', split_axis=3, concat_axis=1, tiled=True)  26.6 us
    unnamed x16, local copies, waits for them, and re-layouts  24.8 us
  transfers between devices with their start and end apart: 2, of which 1 were waited for; matrix products, arithmetic and copies ran while one was open for 55% of the time, Pallas kernels for 0%

profile of v1, /device:TPU:1, one launch (start us, length us, event | category | flops | bytes accessed | tf_op | source)
XLA Modules:
  0.0 638.3 jit_solution(17825601503807326420)
XLA Ops:
  14.3 17.4 %reshape.130 = bf16[2,32,31,4096]{3,2,1,0:T(8,128)(2,1)} reshape(bf16[2,32,126976]{2,1,0:T(8,128)(2,1)} %param.7) | data formatting | bytes 32505856 | tf_op jit(solution)/shard_map/reshape | solution.py:19
  31.8 77.7 %add_convert_fusion = bf16[2,32,16,4096]{3,2,1,0:T(8,128)(2,1)} fusion(bf16[2,32,31,4096]{3,2,1,0:T(8,128)(2,1)} %reshape.130, f32[4096]{0:T(1024)S(1)} %bitcast.112, f32[4096]{0:T(1024)S(1)} %bitcast.113, f32[4096]{0:T(1024)S(1)} %bitcast.99, f32[4096]{0:T(1024)S(1)} %bitcast.100, f32[4096]{0:T(1024)S(1)} %bitcast.101, f32[4096]{0:T(1024)S(1)} %bitcast.102, ...), kind=kLoop, calls=%fused_computation.10 | loop fusion | flops 201326592 | bytes 142868480 | tf_op jit(solution)/shard_map/convert_element_type | solution.py:25
  113.6 9.9 %fusion.47 = f32[512,160]{0,1:T(8,128)S(1)} fusion(bf16[512,4096]{1,0:T(8,128)(2,1)S(1)} %bitcast.85, s32[160]{0:T(256)S(1)} %get-tuple-element.21), kind=kOutput, calls=%fused_computation.67 | convolution fusion | flops 681574400 | bytes 4522624 | tf_op jit(solution)/shard_map/dot_general | solution.py:43
  123.5 10.1 %fusion.48 = f32[512,160]{0,1:T(8,128)S(1)} fusion(bf16[512,4096]{1,0:T(8,128)(2,1)S(1)} %bitcast.89, s32[160]{0:T(256)S(1)} %get-tuple-element.21), kind=kOutput, calls=%fused_computation.68 | convolution fusion | flops 681574400 | bytes 4522624 | tf_op jit(solution)/shard_map/dot_general | solution.py:40
  133.7 10.4 %fusion.53 = bf16[512,160]{0,1:T(8,128)(2,1)S(1)} fusion(f32[512,160]{0,1:T(8,128)S(1)} %fusion.47, bf16[512,4096]{1,0:T(8,128)(2,1)S(1)} %bitcast.90, s32[160]{0:T(256)S(1)} %get-tuple-element.21), kind=kOutput, calls=%fused_computation.73 | convolution fusion | flops 681738240 | bytes 4686464 | tf_op jit(solution)/shard_map/dot_general | solution.py:43
  144.2 12.4 %fusion.54 = bf16[512,160]{0,1:T(8,128)(2,1)S(1)} fusion(f32[512,160]{0,1:T(8,128)S(1)} %fusion.48, bf16[512,4096]{1,0:T(8,128)(2,1)} %bitcast.86, s32[160]{0:T(256)S(1)} %get-tuple-element.21), kind=kOutput, calls=%fused_computation.74 | convolution fusion | flops 681738240 | bytes 4686464 | tf_op jit(solution)/shard_map/dot_general | solution.py:40
  160.7 9.1 %fusion.27 = f32[160,16,2,256]{3,1,2,0:T(8,128)S(1)} fusion(bf16[160,1,16,16,2]{3,2,4,0,1:T(8,128)(2,1)S(1)} %copy.103, f32[160]{0:T(256)S(1)} %convert_multiply_fusion, f32[256,16]{0,1:T(8,128)S(1)} %copy.91, f32[256,16]{0,1:T(8,128)S(1)} %get-tuple-element.47), kind=kOutput, calls=%fused_computation.49 | convolution fusion | flops 43909120 | bytes 5440128 | tf_op jit(solution)/shard_map/sfjp,sbj->sfpb/dot_general | solution.py:72
  169.8 11.8 %fusion.29 = f32[160,16,2,256]{3,1,2,0:T(8,128)} fusion(bf16[160,1,16,16,2]{3,2,4,0,1:T(8,128)(2,1)S(1)} %copy.102, f32[160]{0:T(256)S(1)} %convert_multiply_fusion, f32[256,16]{0,1:T(8,128)S(1)} %copy.91, f32[256,16]{0,1:T(8,128)S(1)} %get-tuple-element.47), kind=kOutput, calls=%fused_computation.50 | convolution fusion | flops 43909120 | bytes 5440128 | tf_op jit(solution)/shard_map/sfjp,sbj->sfpb/dot_general | solution.py:72
  181.5 9.2 %convolution_add_fusion = f32[160,16,2,256]{3,1,2,0:T(8,128)S(1)} fusion(f32[160,16,2,256]{3,1,2,0:T(8,128)S(1)} %fusion.27, bf16[160,1,16,16,2]{3,2,4,0,1:T(8,128)(2,1)S(1)} %copy.102, f32[256,16]{0,1:T(8,128)S(1)} %get-tuple-element.46, f32[160]{0:T(256)S(1)} %convert_multiply_fusion, f32[256,16]{0,1:T(8,128)S(1)} %copy.91), kind=kOutput, calls=%fused_computation.39 | convolution fusion | flops 45219840 | bytes 10683008 | tf_op jit(solution)/shard_map/sfjp,sbj->sfpb/dot_general | solution.py:72
  190.7 7.7 %copy.94 = f32[160,16,2,256]{3,2,1,0:T(2,128)} copy(f32[160,16,2,256]{3,1,2,0:T(8,128)S(1)} %convolution_add_fusion) | data formatting | bytes 10485760 | tf_op jit(solution)/shard_map/add | solution.py:75
  198.4 8.0 %stack.46 = f32[160,1,16,512]{3,2,0,1:T(8,128)} reshape(f32[160,16,2,256]{3,2,1,0:T(2,128)} %copy.94) | data formatting | bytes 10485760 | tf_op jit(solution)/shard_map/stack | solution.py:76
  206.3 12.0 %convolution_subtract_fusion = f32[160,16,2,256]{3,1,2,0:T(8,128)S(1)} fusion(f32[160,16,2,256]{3,1,2,0:T(8,128)} %fusion.29, bf16[160,1,16,16,2]{3,2,4,0,1:T(8,128)(2,1)S(1)} %copy.103, f32[256,16]{0,1:T(8,128)S(1)} %get-tuple-element.46, f32[160]{0:T(256)S(1)} %convert_multiply_fusion, f32[256,16]{0,1:T(8,128)S(1)} %copy.91), kind=kOutput, calls=%fused_computation.40 | convolution fusion | flops 45219840 | bytes 10683008 | tf_op jit(solution)/shard_map/sfjp,sbj->sfpb/dot_general | solution.py:72
  218.4 7.5 %copy.93 = f32[160,16,2,256]{3,2,1,0:T(2,128)} copy(f32[160,16,2,256]{3,1,2,0:T(8,128)S(1)} %convolution_subtract_fusion) | data formatting | bytes 10485760 | tf_op jit(solution)/shard_map/sub | solution.py:74
  225.9 8.0 %stack.45 = f32[160,1,16,512]{3,2,0,1:T(8,128)} reshape(f32[160,16,2,256]{3,2,1,0:T(2,128)} %copy.93) | data formatting | bytes 10485760 | tf_op jit(solution)/shard_map/stack | solution.py:76
  233.8 10.5 %pad_maximum_fusion = f32[160,2,16,512]{3,2,0,1:T(8,128)} fusion(f32[160,1,16,512]{3,2,0,1:T(8,128)} %stack.46, f32[160,1,16,512]{3,2,0,1:T(8,128)} %stack.45), kind=kLoop, calls=%fused_computation.12 | loop fusion | flops 2621440 | bytes 20971520 | tf_op jit(solution)/shard_map/stack | solution.py:76
  244.4 66.0 %fusion.6 = f32[512,1024]{1,0:T(8,128)S(1)} fusion(bf16[512,4096]{1,0:T(8,128)(2,1)} %bitcast.87, s32[1024]{0:T(1024)S(1)} %iota_add_fusion), kind=kOutput, calls=%fused_computation.14 | convolution fusion | flops 4362076160 | bytes 6295552 | tf_op jit(solution)/shard_map/dot_general | solution.py:43
  310.4 63.5 %fusion.7 = f32[512,1024]{1,0:T(8,128)S(1)} fusion(bf16[512,4096]{1,0:T(8,128)(2,1)S(1)} %bitcast.91, s32[1024]{0:T(1024)S(1)} %iota_add_fusion), kind=kOutput, calls=%fused_computation.15 | convolution fusion | flops 4362076160 | bytes 6295552 | tf_op jit(solution)/shard_map/dot_general | solution.py:40
  373.9 64.1 %subtract_convert_fusion = bf16[512,1024]{1,0:T(8,128)(2,1)S(1)} fusion(f32[512,1024]{1,0:T(8,128)S(1)} %fusion.6, bf16[512,4096]{1,0:T(8,128)(2,1)S(1)} %bitcast.92, s32[1024]{0:T(1024)S(1)} %iota_add_fusion), kind=kOutput, calls=%fused_computation.45 | convolution fusion | flops 4363124736 | bytes 7344128 | tf_op jit(solution)/shard_map/dot_general | solution.py:43
  438.0 64.1 %add_convert_fusion.1 = bf16[512,1024]{1,0:T(8,128)(2,1)S(1)} fusion(f32[512,1024]{1,0:T(8,128)S(1)} %fusion.7, bf16[512,4096]{1,0:T(8,128)(2,1)S(1)} %bitcast.88, s32[1024]{0:T(1024)S(1)} %iota_add_fusion), kind=kOutput, calls=%fused_computation.46 | convolution fusion | flops 4363124736 | bytes 7344128 | tf_op jit(solution)/shard_map/dot_general | solution.py:40
  502.3 14.0 %copy.83 = bf16[2,32,16,1024]{1,2,0,3:T(8,128)(2,1)} copy(bf16[2,32,16,1024]{3,2,1,0:T(8,128)(2,1)S(1)} %pad_maximum_fusion.1) | data formatting | bytes 4194304 | tf_op jit(solution)/shard_map/stack | solution.py:46
  516.3 13.3 %reshape.141 = bf16[32,2,16384]{2,1,0:T(2,128)(2,1)} reshape(bf16[1024,2,16,32]{3,2,1,0:T(8,128)(2,1)} %bitcast.82) | data formatting | bytes 4194304
  529.6 9.6 %all-to-all-start = ((bf16[32,2,16384]{2,1,0:T(2,128)(2,1)}), bf16[32,2,16384]{2,1,0:T(2,128)(2,1)S(1)}, u32[]{:S(2)}, u32[]{:S(2)}) async-start(bf16[32,2,16384]{2,1,0:T(2,128)(2,1)} %reshape.141), calls=%async_computation | async-start | bytes 4194304 | tf_op jit(solution)/shard_map/all_to_all | solution.py:92
  540.4 26.6 %all-to-all-done = bf16[32,2,16384]{2,1,0:T(2,128)(2,1)S(1)} async-done(((bf16[32,2,16384]{2,1,0:T(2,128)(2,1)}), bf16[32,2,16384]{2,1,0:T(2,128)(2,1)S(1)}, u32[]{:S(2)}, u32[]{:S(2)}) %all-to-all-start) | async-done | bytes 2097184 | tf_op jit(solution)/shard_map/all_to_all | solution.py:92
  573.4 19.2 %copy.99 = bf16[2,32,16,32,32]{4,3,2,1,0:T(8,128)(2,1)} copy(bf16[2,32,16,32,32]{1,2,0,4,3:T(8,128)(2,1)} %bitcast.83) | data formatting | bytes 4194304 | tf_op jit(solution)/shard_map/all_to_all | solution.py:92
  (48 shorter events, 61.0 us)
Async XLA Ops:
  7.2 622.1 %all-reduce.3.cloned.1.call-start = ((), (), s32[]{:S(2)}) async-start(), calls=%async_computation.1 | async-start | bytes 20971520
  113.6 9.9 %copy-start = (bf16[1,32,16,4096]{3,2,1,0:T(8,128)(2,1)}, bf16[1,32,16,4096]{3,2,1,0:T(8,128)(2,1)S(1)}, u32[]{:S(2)}) copy-start(bf16[1,32,16,4096]{3,2,1,0:T(8,128)(2,1)S(1)} %get-tuple-element.25) | copy-start | bytes 12582916
  113.6 20.1 %copy-start.2 = (bf16[1,32,16,4096]{3,2,1,0:T(8,128)(2,1)}, bf16[1,32,16,4096]{3,2,1,0:T(8,128)(2,1)S(1)}, u32[]{:S(2)}) copy-start(bf16[1,32,16,4096]{3,2,1,0:T(8,128)(2,1)S(1)} %get-tuple-element.24) | copy-start | bytes 12582916
  244.4 66.0 %copy-start.3 = (bf16[1,32,16,4096]{3,2,1,0:T(8,128)(2,1)S(1)}, bf16[1,32,16,4096]{3,2,1,0:T(8,128)(2,1)}, u32[]{:S(2)}) copy-start(bf16[1,32,16,4096]{3,2,1,0:T(8,128)(2,1)} %copy-done.2) | copy-start | bytes 12582916
  373.9 64.1 %copy-start.1 = (bf16[1,32,16,4096]{3,2,1,0:T(8,128)(2,1)S(1)}, bf16[1,32,16,4096]{3,2,1,0:T(8,128)(2,1)}, u32[]{:S(2)}) copy-start(bf16[1,32,16,4096]{3,2,1,0:T(8,128)(2,1)} %copy-done) | copy-start | bytes 12582916
  529.6 9.6 %copy-start.4 = (u32[128]{0:T(128)S(1)}, u32[128]{0:T(128)}, u32[]{:S(2)}) copy-start(u32[128]{0:T(128)} %constant.54) | copy-start | bytes 1540
  529.6 37.4 %all-to-all-start = ((bf16[32,2,16384]{2,1,0:T(2,128)(2,1)}), bf16[32,2,16384]{2,1,0:T(2,128)(2,1)S(1)}, u32[]{:S(2)}, u32[]{:S(2)}) async-start(bf16[32,2,16384]{2,1,0:T(2,128)(2,1)} %reshape.141), calls=%async_computation | async-start | bytes 4194304 | tf_op jit(solution)/shard_map/all_to_all | solution.py:92
Sparse Core Ops, SparseCore 0:
  244.5 129.2 all-reduce.2

commit v2 on v0

v2 whole, which is shorter than its diff:
```python
import math

import jax
import jax.numpy as jnp
from jax import lax
from jax.experimental import pallas as pl
from jax.experimental.pallas import tpu as pltpu
from jax.sharding import PartitionSpec as P

NCH = 4096
FRAMES = 16
TAPS = 16
SLOTS = 160
BAND = 1024
GROUPS = 32
PER_DEV = 5
QUARTER = 1024
SIG = 16
SIGNALS = 1024
ROWS = 80
NT = (((1,), (1,)), ((), ()))
F32 = jnp.float32
BF16 = jnp.bfloat16
VMEM_LIMIT = 56 << 20
MESH = pl.DeviceIdType.MESH
PIECES = ((0, 32), (32, 16), (48, 16), (64, 16))


def sincos_turns(turns):
    quarter = jnp.floor(turns * 4.0 + 0.5)
    x = (turns - quarter * 0.25) * (2.0 * math.pi)
    z = x * x
    sin_x = x * (1.0 + z * (-1.0 / 6 + z * (1.0 / 120 + z * (-1.0 / 5040 + z * (1.0 / 362880)))))
    cos_x = 1.0 + z * (-0.5 + z * (1.0 / 24 + z * (-1.0 / 720 + z * (1.0 / 40320))))
    which = quarter.astype(jnp.int32) & 3
    odd = (which & 1) == 1
    s = jnp.where(odd, cos_x, sin_x)
    c = jnp.where(odd, sin_x, cos_x)
    s = jnp.where(which >= 2, -s, s)
    c = jnp.where((which == 1) | (which == 2), -c, c)
    return s, c


def fill_tables(chan_ref, table):
    @pl.loop(0, chan_ref.shape[0] // 32)
    def _(block):
        at = pl.ds(pl.multiple_of(block * 32, 32), 32)
        wide = jnp.broadcast_to(chan_ref[at, :], (32, 128))
        lane = lax.broadcasted_iota(jnp.int32, (32, 128), 1)
        s, c = sincos_turns(((lane * wide) & (NCH - 1)).astype(F32) * (1.0 / NCH))
        s_step, c_step = sincos_turns(((128 * wide) & (NCH - 1)).astype(F32) * (1.0 / NCH))
        s, c = s * (1.0 / 64), c * (1.0 / 64)
        for tile in range(QUARTER // 128):
            lanes = slice(tile * 128, tile * 128 + 128)
            table[0, at, lanes] = c.astype(BF16)
            table[1, at, lanes] = s.astype(BF16)
            s, c = s * c_step + c * s_step, c * c_step - s * s_step


def filter_group(volts, proto_ref, filt, spec):
    @pl.loop(0, QUARTER // 128)
    def _(tile):
        @pl.loop(0, 4)
        def _(n1):
            base = pl.multiple_of(n1 * QUARTER + tile * 128, 128)
            taps = [
                jnp.broadcast_to(proto_ref[t : t + 1, pl.ds(base, 128)], (SIG, 128))
                for t in range(TAPS)
            ]
            for part in range(2):
                for half in range(2):
                    acc = [None] * 8
                    for u in range(8 + TAPS - 1):
                        at = pl.multiple_of((half * 8 + u) * NCH + base, 128)
                        v = volts[part, :, pl.ds(at, 128)].astype(F32)
                        for f in range(8):
                            t = u - f
                            if 0 <= t < TAPS:
                                term = taps[t] * v
                                acc[f] = term if acc[f] is None else acc[f] + term
                    for f in range(8):
                        filt[part * 4 + n1, half * 8 + f] = acc[f]

        lanes = pl.ds(pl.multiple_of(tile * 128, 128), 128)
        for f in range(FRAMES):
            re = [filt[n1, f] for n1 in range(4)]
            im = [filt[4 + n1, f] for n1 in range(4)]
            ar, ai = re[0] + re[2], im[0] + im[2]
            br, bi = re[0] - re[2], im[0] - im[2]
            cr, ci = re[1] + re[3], im[1] + im[3]
            dr, di = re[1] - re[3], im[1] - im[3]
            outs = [(ar + cr, ai + ci), (br + di, bi - dr), (ar - cr, ai - ci), (br - di, bi + dr)]
            for k1 in range(4):
                for part in range(2):
                    at = part * 256 + f * SIG
                    spec[k1, at : at + SIG, lanes] = outs[k1][part].astype(BF16)


def by_group(re, im):
    joined = jnp.concatenate([re.reshape(32, 8, 256), im.reshape(32, 8, 256)], axis=1)
    return joined.astype(BF16)


def exchange_kernel(
    volts_hbm, proto_ref, chan_ref, recv_ref,
    volts, table, filt, spec, send, load_sem, own_sem, send_sem, recv_sem,
):
    n = GROUPS
    me = lax.axis_index("st")

    def load(g):
        src = volts_hbm.at[:, pl.ds(g * SIG, SIG), :]
        return pltpu.make_async_copy(src, volts.at[g], load_sem.at[g])

    load(0).start()
    load(1).start()
    barrier = pltpu.get_barrier_semaphore()

    @pl.loop(1, n)
    def _(d):
        there = lax.rem(me + d, n)
        pl.semaphore_signal(barrier, inc=1, device_id={"st": there}, device_id_type=MESH)

    fill_tables(chan_ref, table)
    pl.semaphore_wait(barrier, n - 1)

    def own(g):
        return pltpu.make_async_copy(send.at[g, me], recv_ref.at[g, me], own_sem.at[g])

    def remote(g, piece, there):
        rows = pl.ds(*PIECES[piece])
        return pltpu.make_async_remote_copy(
            src_ref=send.at[g, there, rows],
            dst_ref=recv_ref.at[g, me, rows],
            send_sem=send_sem.at[g, piece],
            recv_sem=recv_sem.at[g, piece],
            device_id={"st": there},
            device_id_type=MESH,
        )

    def start(g, piece):
        @pl.loop(1, n)
        def _(d):
            remote(g, piece, lax.rem(me + d, n)).start()

    @pl.loop(0, 2)
    def _(g):
        src = volts_hbm.at[:, pl.ds(g * SIG, SIG), :]
        pltpu.make_async_copy(src, volts.at[g], load_sem.at[g]).wait()
        filter_group(volts.at[g], proto_ref, filt, spec)

        def both(k1, rows):
            a = spec[k1]
            c = lax.dot_general(table[0, rows], a, NT, preferred_element_type=F32)
            s = lax.dot_general(table[1, rows], a, NT, preferred_element_type=F32)
            return c[:, :256] + s[:, 256:], c[:, 256:] - s[:, :256]

        chan = chan_ref[1024:1280, :]
        beam_re = jnp.zeros((256, 256), F32)
        beam_im = jnp.zeros((256, 256), F32)
        for k1 in range(4):
            re, im = both(k1, slice(1024, 1280))
            mine = (chan & 3) == k1
            beam_re = jnp.where(mine, re, beam_re)
            beam_im = jnp.where(mine, im, beam_im)
        row = lax.broadcasted_iota(jnp.int32, (256, 256), 0)
        col = lax.broadcasted_iota(jnp.int32, (256, 256), 1)
        turn = (row == (col & 15) * 16 + (col >> 4)).astype(F32).astype(BF16)
        joined = by_group(beam_re, beam_im).reshape(512, 256)
        turned = jnp.dot(joined, turn, preferred_element_type=F32)
        send[g, :, 0:16, :] = turned.astype(BF16).reshape(32, 16, 256)
        for k1 in range(4):
            re, im = both(k1, slice(k1 * 256, k1 * 256 + 256))
            send[g, :, 16 + k1 * 16 : 32 + k1 * 16, :] = by_group(re, im)
            start(g, k1)
        own(g).start()

    for g in range(2):
        own(g).wait()
        for piece in range(4):
            rows = pl.ds(*PIECES[piece])
            others = pl.ds(0, n - 1)
            all_of = pltpu.make_async_remote_copy(
                src_ref=send.at[g, others, rows],
                dst_ref=recv_ref.at[g, others, rows],
                send_sem=send_sem.at[g, piece],
                recv_sem=recv_sem.at[g, piece],
                device_id={"st": lax.rem(me + 1, n)},
                device_id_type=MESH,
            )
            all_of.wait_send()
            all_of.wait_recv()


def exchange(volts, prototype, chan):
    vmem = pl.BlockSpec(memory_space=pltpu.VMEM)
    hbm = pl.BlockSpec(memory_space=pl.ANY)
    return pl.pallas_call(
        exchange_kernel,
        out_shape=jax.ShapeDtypeStruct((2, GROUPS, ROWS, 256), BF16),
        in_specs=[hbm, vmem, vmem],
        out_specs=hbm,
        scratch_shapes=[
            pltpu.VMEM((2, 2, SIG, volts.shape[2]), BF16),
            pltpu.VMEM((2, chan.shape[0], QUARTER), BF16),
            pltpu.VMEM((8, FRAMES, SIG, 128), F32),
            pltpu.VMEM((4, 512, QUARTER), BF16),
            pltpu.VMEM((2, GROUPS, ROWS, 256), BF16),
            pltpu.SemaphoreType.DMA((2,)),
            pltpu.SemaphoreType.DMA((2,)),
            pltpu.SemaphoreType.DMA((2, 4)),
            pltpu.SemaphoreType.DMA((2, 4)),
        ],
        compiler_params=pltpu.CompilerParams(
            vmem_limit_bytes=VMEM_LIMIT, collective_id=0, has_side_effects=True
        ),
        name="channelise",
    )(volts, prototype, chan)


def correlate_kernel(recv_ref, out_ref, plain, turned):
    @pl.when(pl.program_id(0) == 0)
    def _():
        @pl.loop(0, 32)
        def _(src):
            for chunk in range(2):
                block = recv_ref[chunk, src, 16:80, :].astype(F32)
                parts = [block[:, :128], block[:, 128:]]
                stacked = jnp.concatenate(parts, axis=0)
                by_part = stacked.reshape(8, 2, 8, 128)
                swapped = jnp.stack([by_part[:, 1], -by_part[:, 0]], axis=1).reshape(128, 128)
                at = pl.ds(pl.multiple_of(src * 32 + chunk * SIG, SIG), SIG)
                for x, dest in ((stacked, plain), (swapped, turned)):
                    t = x.T.astype(BF16)
                    for f in range(8):
                        dest[at, f * 128 : f * 128 + 128] = t[f * 16 : f * 16 + 16]

    rows = pl.ds(pl.multiple_of(pl.program_id(0) * 256, 256), 256)
    whole = plain[...]
    scale = 1.0 / 512
    out_ref[0, 0, 0] = lax.dot_general(plain[rows, :], whole, NT, preferred_element_type=F32) * scale
    out_ref[1, 0, 0] = lax.dot_general(turned[rows, :], whole, NT, preferred_element_type=F32) * scale


def correlate(recv):
    once = pl.Buffered(1)
    whole = pl.BlockSpec((2, GROUPS, ROWS, 256), lambda i: (0, 0, 0, 0), pipeline_mode=once)
    return pl.pallas_call(
        correlate_kernel,
        grid=(4,),
        out_shape=jax.ShapeDtypeStruct((2, 1, 1, SIGNALS, SIGNALS), F32),
        in_specs=[whole],
        out_specs=pl.BlockSpec((2, 1, 1, 256, SIGNALS), lambda i: (0, 0, 0, i, 0)),
        scratch_shapes=[pltpu.VMEM((SIGNALS, 1024), BF16), pltpu.VMEM((SIGNALS, 1024), BF16)],
        compiler_params=pltpu.CompilerParams(vmem_limit_bytes=VMEM_LIMIT),
        name="correlate",
    )(recv)


def beams_kernel(x_ref, station_ref, delay_ref, gain_ref, chan_ref, filled_ref, out_ref):
    listed = station_ref.shape[1]
    row = lax.broadcasted_iota(jnp.int32, (512, listed), 0)
    station = (row & 31) * 16 + ((row >> 5) & 1) * 8 + (row >> 6)
    select = (station == station_ref[...]).astype(F32).astype(BF16)
    x = []
    for r in range(2 * PER_DEV):
        t = x_ref[r].astype(F32).T.astype(BF16)
        x.append(jnp.concatenate([t[s * 32 : s * 32 + 32] for s in range(8)], axis=1))
    picked = jnp.dot(jnp.concatenate(x, axis=0), select, preferred_element_type=F32).astype(BF16)
    scaling = gain_ref[...] * (1.0 / math.sqrt(listed))
    for slot in range(PER_DEV):
        turns = delay_ref[...] * (chan_ref[0, slot].astype(F32) * (1.0 / NCH))
        turns = turns - jnp.floor(turns)
        s, c = sincos_turns(turns)
        level = scaling * filled_ref[0, slot].astype(F32)
        w_re, w_im = (level * c).astype(BF16), (-level * s).astype(BF16)
        at = slot * 64
        pair = picked[at : at + 64]
        with_re = lax.dot_general(pair, w_re, NT, preferred_element_type=F32)
        with_im = lax.dot_general(pair, w_im, NT, preferred_element_type=F32)
        out_re = with_re[:32] - with_im[32:]
        out_im = with_re[32:] + with_im[:32]
        for part, out in enumerate((out_re, out_im)):
            out_ref[0, slot, part, :, 0:256] = out[:16]
            out_ref[0, slot, part, :, 256:512] = out[16:]


def beams(x, station_index, delays, gains, chan, filled):
    smem = pl.BlockSpec(memory_space=pltpu.SMEM)
    vmem = pl.BlockSpec(memory_space=pltpu.VMEM)
    return pl.pallas_call(
        beams_kernel,
        out_shape=jax.ShapeDtypeStruct((1, PER_DEV, 2, FRAMES, 512), F32),
        in_specs=[vmem, vmem, vmem, vmem, smem, smem],
        out_specs=vmem,
        compiler_params=pltpu.CompilerParams(vmem_limit_bytes=VMEM_LIMIT),
        name="beams",
    )(x, station_index, delays, gains, chan, filled)


def body(volts, prototype, beam_channels, station_index, delays, gains, assign):
    sb_here = lax.axis_index("sb")
    st_here = lax.axis_index("st")
    owners = assign[:, 0]
    order = jnp.arange(owners.shape[0], dtype=jnp.int32)
    matches = (owners == sb_here).astype(jnp.int32)
    position = jnp.sum((order[None, :] < order[:, None]).astype(jnp.int32) * matches[None, :], axis=1)
    row = jnp.arange(256, dtype=jnp.int32)
    slot = jnp.where((row & 7) < PER_DEV, (row >> 3) * PER_DEV + (row & 7), -1)
    picker = matches[None, :] * (position[None, :] == slot[:, None]).astype(jnp.int32)
    filled = jnp.sum(picker, axis=1)
    slot_channel = jnp.sum(picker * beam_channels[None, :], axis=1)
    line = jnp.arange(1024, dtype=jnp.int32)
    main = sb_here * BAND + (line & 255) * 4 + (line >> 8)
    recv = exchange(volts, prototype, jnp.concatenate([main, slot_channel])[:, None])
    visibility = correlate(recv)
    x = recv[:, :, 0:16].reshape(2, 32, 2, 8, 256)[:, :, :, :PER_DEV]
    x = x.transpose(3, 2, 0, 1, 4).reshape(2 * PER_DEV, 64, 256)
    mine = lax.dynamic_slice_in_dim(slot_channel, st_here * 8, 8)[None]
    there = lax.dynamic_slice_in_dim(filled, st_here * 8, 8)[None]
    beam_out = beams(x, station_index[None], delays, gains, mine, there)
    return (visibility, beam_out)


def solution(mesh):
    in_specs = (P(None, "st", None), P(), P(), P(), P(), P(), P())
    out_specs = (P(None, "sb", "st", None, None), P("sb", "st", None, None, None))
    return jax.shard_map(body, mesh=mesh, in_specs=in_specs, out_specs=out_specs, check_vma=False)
```

time: 649 us -> 85.6 us (0.13); the launches traced: 639 us -> 85.3 us
  matrix products: 347 us -> 0 us
  local copies, waits for them, and re-layouts: 142 us -> 3.66 us
  other arithmetic: 98 us -> 1.78 us
  Pallas kernels: 0 us -> 79.2 us
  waiting for transfers between devices: 26.6 us -> 0 us
  between operations: 15.2 us -> 0.66 us
  starting transfers between devices: 9.6 us -> 0 us
    dot_general x14 -> x0, matrix products: 347 us -> none  [the longest x2 76.7 us: transform(): jnp.dot(flat_rows[1], sin_t, preferred_element_type=jnp.float32)]
    pallas_call x0 -> x3, Pallas kernels: none -> 79.2 us  [the longest x1 62.8 us: exchange(): pl.pallas_call(exchange_kernel, out_shape=jax.ShapeDtypeStruct((2, GROUPS...]
    convert_element_type x3 -> x0, other arithmetic: 78.5 us -> none  [the longest x1 77.7 us: polyphase(): return summed.astype(jnp.bfloat16)]
    another operation x6 -> x0, local copies, waits for them, and re-layouts: 30.3 us -> none  [the longest x2 15.9 us: combine(): stacked = jnp.stack([out_re, out_im], axis=1)]
    all_to_all x1 -> x0, waiting for transfers between devices: 26.6 us -> none  [body(): lax.all_to_all(spectra, 'st', split_axis=3, concat_axis=1, tiled=True)]
    unnamed x16 -> x1, local copies, waits for them, and re-layouts: 24.8 us -> 0.84 us
    slice x7 -> x0, local copies, waits for them, and re-layouts: 21.6 us -> none  [the longest x3 15.1 us: correlate(): stacked = jnp.concatenate([grouped[0], grouped[1]], axis=1)]
    all_to_all x1 -> x0, local copies, waits for them, and re-layouts: 19.2 us -> none  [body(): lax.all_to_all(spectra, 'st', split_axis=3, concat_axis=1, tiled=True)]
  transfers between devices with their start and end apart: 2 -> 0, of which waited for: 1 -> 0; matrix products, arithmetic and copies ran while one was open for 54% -> 0% of each run, Pallas kernels for 0% -> 0%
where the time goes in v2:
time: 85.6 us; the launch traced here: 85.3 us
  Pallas kernels  79.2 us (93%)
  local copies, waits for them, and re-layouts  3.66 us (4%)
  other arithmetic  1.78 us (2%)
    pallas_call x1, Pallas kernels, exchange(): pl.pallas_call(exchange_kernel, out_shape=jax.ShapeDtypeStruct((2, GROUPS...  62.8 us
    pallas_call x1, Pallas kernels, correlate(): pl.pallas_call(correlate_kernel, grid=(4,), out_shape=jax.ShapeDtypeStruc...  11.8 us
    pallas_call x1, Pallas kernels, beams(): pl.pallas_call(beams_kernel, out_shape=jax.ShapeDtypeStruct((1, PER_DEV,...  4.6 us

profile of v2, /device:TPU:1, one launch (start us, length us, event | category | flops | bytes accessed | tf_op | source)
XLA Modules:
  0.0 85.3 jit_solution(10100771290439151560)
XLA Ops:
  0.6 0.7 fusion.1
  1.3 0.1 select_reduce_fusion
  1.5 0.9 %select_reduce_fusion.1 = (s32[256]{0:T(256)S(1)}, s32[256]{0:T(256)S(1)}) fusion(s32[384]{0:T(512)S(1)} %fusion.1, s32[384]{0:T(512)S(1)} %select_reduce_fusion, s32[256]{0:T(256)S(1)} %compare_select_fusion, s32[384]{0:T(512)} %param.9), kind=kLoop, calls=%fused_computation.3 | loop fusion | flops 491008 | bytes 7680 | tf_op jit(solution)/shard_map/reduce_sum | solution.py:311
  2.4 0.7 dynamic-slice_bitcast_fusion
  3.1 1.1 %broadcast_in_dim.28.chan_ref = s32[1280,1]{1,0:T(8,128)} reshape(s32[1280]{0:T(1024)S(1)} %pad_add_fusion) | data formatting | bytes 10240 | tf_op jit(solution)/shard_map/broadcast_in_dim | solution.py:315
  4.2 62.8 %channelise.1.recv_ref = bf16[2,32,80,256]{3,2,1,0:T(8,128)(2,1)} custom-call(bf16[2,32,126976]{2,1,0:T(8,128)(2,1)} %volts_hbm.1, f32[16,4096]{1,0:T(8,128)} %proto_ref.1, s32[1280,1]{1,0:T(8,128)} %broadcast_in_dim.28.chan_ref), custom_call_target="tpu_custom_call" | custom-call | tf_op jit(solution)/shard_map/channelise/pallas_call | solution.py:198
  67.0 1.1 %slice_bitcast_fusion = bf16[2,32,2,8,256]{4,3,2,1,0:T(8,128)(2,1)S(1)} fusion(bf16[2,32,80,256]{3,2,1,0:T(8,128)(2,1)} %channelise.1.recv_ref), kind=kLoop, calls=%fused_computation.2 | loop fusion | bytes 1048576 | tf_op jit(solution)/shard_map/reshape | solution.py:317
  68.1 0.8 copy.14
  68.9 4.6 %beams.1 = f32[1,5,2,16,512]{4,3,2,1,0:T(8,128)} custom-call(bf16[10,64,256]{2,1,0:T(8,128)(2,1)} %bitcast.12, s32[1,256]{1,0:T(1,128)} %bitcast.13, f32[256,256]{1,0:T(8,128)} %delay_ref.1, f32[256,256]{1,0:T(8,128)} %gain_ref.1, s32[1,8]{1,0:T(1,128)} %get-tuple-element.5.chan_ref, s32[1,8]{1,0:T(1,128)} %get-tuple-element.4.filled_ref), custom_call_target="tpu_custom_call" | custom-call | tf_op jit(solution)/shard_map/beams/pallas_call | solution.py:291
  73.5 11.8 %correlate.1 = f32[2,1,1,1024,1024]{4,3,2,1,0:T(8,128)} custom-call(bf16[2,32,80,256]{3,2,1,0:T(8,128)(2,1)} %channelise.1.recv_ref), custom_call_target="tpu_custom_call" | custom-call | tf_op jit(solution)/shard_map/correlate/pallas_call | solution.py:248
  (3 shorter events, 0.0 us)

commit v3 on v2

v3 whole, which is shorter than its diff:
```python
import math

import jax
import jax.numpy as jnp
from jax import lax
from jax.experimental import pallas as pl
from jax.experimental.pallas import tpu as pltpu
from jax.sharding import PartitionSpec as P

NCH = 4096
FRAMES = 16
TAPS = 16
SLOTS = 160
BAND = 1024
GROUPS = 32
PER_DEV = 5
QUARTER = 1024
SIG = 16
SIGNALS = 1024
ROWS = 80
NT = (((1,), (1,)), ((), ()))
F32 = jnp.float32
BF16 = jnp.bfloat16
VMEM_LIMIT = 56 << 20
MESH = pl.DeviceIdType.MESH
PIECES = ((0, 48), (48, 32))
HALF = 8
CHIPS = ((2, 2), (1, 2), (2, 1), (3, 2), (2, 3), (0, 2), (2, 0), (1, 1), (3, 3), (1, 3), (3, 1), (0, 1), (3, 0), (0, 3), (1, 0))
ORDER = tuple((z, x, c) for z, x in CHIPS for c in range(2)) + ((0, 0, 1),)


def sincos_turns(turns):
    quarter = jnp.floor(turns * 4.0 + 0.5)
    x = (turns - quarter * 0.25) * (2.0 * math.pi)
    z = x * x
    sin_x = x * (1.0 + z * (-1.0 / 6 + z * (1.0 / 120 + z * (-1.0 / 5040 + z * (1.0 / 362880)))))
    cos_x = 1.0 + z * (-0.5 + z * (1.0 / 24 + z * (-1.0 / 720 + z * (1.0 / 40320))))
    which = quarter.astype(jnp.int32) & 3
    odd = (which & 1) == 1
    s = jnp.where(odd, cos_x, sin_x)
    c = jnp.where(odd, sin_x, cos_x)
    s = jnp.where(which >= 2, -s, s)
    c = jnp.where((which == 1) | (which == 2), -c, c)
    return s, c


def fill_tables(chan_ref, table):
    @pl.loop(0, chan_ref.shape[0] // 32)
    def _(block):
        at = pl.ds(pl.multiple_of(block * 32, 32), 32)
        wide = jnp.broadcast_to(chan_ref[at, :], (32, 128))
        lane = lax.broadcasted_iota(jnp.int32, (32, 128), 1)
        s, c = sincos_turns(((lane * wide) & (NCH - 1)).astype(F32) * (1.0 / NCH))
        s_step, c_step = sincos_turns(((128 * wide) & (NCH - 1)).astype(F32) * (1.0 / NCH))
        s, c = s * (1.0 / 64), c * (1.0 / 64)
        which = block // 8
        cos_at = pl.ds(pl.multiple_of((block % 8) * 32, 32), 32)
        sin_at = pl.ds(pl.multiple_of((block % 8) * 32 + 256, 32), 32)
        for tile in range(QUARTER // 128):
            lanes = slice(tile * 128, tile * 128 + 128)
            table[which, cos_at, lanes] = c.astype(BF16)
            table[which, sin_at, lanes] = s.astype(BF16)
            s, c = s * c_step + c * s_step, c * c_step - s * s_step


def filter_frames(volts, half, proto_ref, filt, spec):
    @pl.loop(0, QUARTER // 128)
    def _(tile):
        @pl.loop(0, 4)
        def _(n1):
            base = pl.multiple_of(n1 * QUARTER + tile * 128, 128)
            taps = [
                jnp.broadcast_to(proto_ref[t : t + 1, pl.ds(base, 128)], (SIG, 128))
                for t in range(TAPS)
            ]
            for part in range(2):
                acc = [None] * HALF
                for u in range(HALF + TAPS - 1):
                    at = pl.multiple_of((half * HALF + u) * NCH + base, 128)
                    v = volts[part, :, pl.ds(at, 128)].astype(F32)
                    for f in range(HALF):
                        t = u - f
                        if 0 <= t < TAPS:
                            term = taps[t] * v
                            acc[f] = term if acc[f] is None else acc[f] + term
                for f in range(HALF):
                    filt[part * 4 + n1, f] = acc[f]

        lanes = pl.ds(pl.multiple_of(tile * 128, 128), 128)
        for f in range(HALF):
            re = [filt[n1, f] for n1 in range(4)]
            im = [filt[4 + n1, f] for n1 in range(4)]
            ar, ai = re[0] + re[2], im[0] + im[2]
            br, bi = re[0] - re[2], im[0] - im[2]
            cr, ci = re[1] + re[3], im[1] + im[3]
            dr, di = re[1] - re[3], im[1] - im[3]
            outs = [(ar + cr, ai + ci), (br + di, bi - dr), (ar - cr, ai - ci), (br - di, bi + dr)]
            for k1 in range(4):
                for part in range(2):
                    at = part * 128 + f * SIG
                    spec[k1, at : at + SIG, lanes] = outs[k1][part].astype(BF16)


def by_group(re, im):
    joined = jnp.concatenate([re.reshape(32, 8, 128), im.reshape(32, 8, 128)], axis=1)
    return joined.astype(BF16)


def exchange_kernel(
    volts_hbm, proto_ref, chan_ref, delay_ref, gain_ref, mine_ref, filled_ref,
    plain_hbm, turned_hbm, beam_hbm, weight_hbm,
    volts, table, filt, spec, send, recv, plain, turned, weight,
    load_sem, own_sem, send_sem, recv_sem, out_sem,
):
    n = GROUPS
    me = lax.axis_index("st")

    def load(g):
        src = volts_hbm.at[:, pl.ds(g * SIG, SIG), :]
        return pltpu.make_async_copy(src, volts.at[g], load_sem.at[g])

    load(0).start()
    barrier = pltpu.get_barrier_semaphore()

    @pl.loop(1, n)
    def _(d):
        there = lax.rem(me + d, n)
        pl.semaphore_signal(barrier, inc=1, device_id={"st": there}, device_id_type=MESH)

    fill_tables(chan_ref, table)
    load(1).start()
    pl.semaphore_wait(barrier, n - 1)

    def own(q):
        return pltpu.make_async_copy(send.at[q, me], recv.at[q, me], own_sem.at[q])

    def remote(q, piece, there):
        rows = pl.ds(*PIECES[piece])
        return pltpu.make_async_remote_copy(
            src_ref=send.at[q, there, rows],
            dst_ref=recv.at[q, me, rows],
            send_sem=send_sem.at[q, piece],
            recv_sem=recv_sem.at[q, piece],
            device_id={"st": there},
            device_id_type=MESH,
        )

    def start(q, piece):
        plane, column, core = me // 8, (me // 2) % 4, me % 2
        for dz, dx, dc in ORDER:
            there = ((plane + dz) % 4) * 8 + ((column + dx) % 4) * 2 + (core + dc) % 2
            remote(q, piece, there).start()

    @pl.loop(0, 4)
    def _(step):
        g, half = step // 2, step % 2
        q = half * 2 + g

        @pl.when(half == 0)
        def _():
            src = volts_hbm.at[:, pl.ds(g * SIG, SIG), :]
            pltpu.make_async_copy(src, volts.at[g], load_sem.at[g]).wait()

        filter_frames(volts.at[g], half, proto_ref, filt, spec)

        def both(k1, which):
            t = lax.dot_general(table[which], spec[k1], NT, preferred_element_type=F32)
            c, s = t[:256], t[256:]
            return c[:, :128] + s[:, 128:], c[:, 128:] - s[:, :128]

        chan = chan_ref[1024:1280, :]
        beam_re = jnp.zeros((256, 128), F32)
        beam_im = jnp.zeros((256, 128), F32)
        for k1 in range(4):
            re, im = both(k1, 4)
            mine = (chan & 3) == k1
            beam_re = jnp.where(mine, re, beam_re)
            beam_im = jnp.where(mine, im, beam_im)
        row = lax.broadcasted_iota(jnp.int32, (128, 128), 0)
        col = lax.broadcasted_iota(jnp.int32, (128, 128), 1)
        turn = (row == (col & 7) * 16 + (col >> 3)).astype(F32).astype(BF16)
        joined = by_group(beam_re, beam_im).reshape(512, 128)
        placed = jnp.dot(joined, turn, preferred_element_type=F32)
        send[q, :, 0:16, :] = placed.astype(BF16).reshape(32, 16, 128)
        for k1 in range(4):
            re, im = both(k1, k1)
            send[q, :, 16 + k1 * 16 : 32 + k1 * 16, :] = by_group(re, im)
            if k1 % 2 == 1:
                start(q, k1 // 2)
        own(q).start()

    @pl.loop(0, delay_ref.shape[0] // 32)
    def _(block):
        at = pl.ds(pl.multiple_of(block * 32, 32), 32)
        scaling = gain_ref[at, :] * (1.0 / math.sqrt(gain_ref.shape[1]))
        for slot in range(PER_DEV):
            turns = delay_ref[at, :] * (mine_ref[0, slot].astype(F32) * (1.0 / NCH))
            turns = turns - jnp.floor(turns)
            s, c = sincos_turns(turns)
            level = scaling * filled_ref[0, slot].astype(F32)
            weight[slot, 0, at, :] = (level * c).astype(BF16)
            weight[slot, 1, at, :] = (-level * s).astype(BF16)

    copies = [pltpu.make_async_copy(weight, weight_hbm, out_sem.at[0])]
    copies[0].start()
    for g in range(2):
        for q in (g, 2 + g):
            own(q).wait()
            for piece in range(len(PIECES)):
                rows = pl.ds(*PIECES[piece])
                others = pl.ds(0, n - 1)
                all_of = pltpu.make_async_remote_copy(
                    src_ref=send.at[q, others, rows],
                    dst_ref=recv.at[q, others, rows],
                    send_sem=send_sem.at[q, piece],
                    recv_sem=recv_sem.at[q, piece],
                    device_id={"st": lax.rem(me + 1, n)},
                    device_id_type=MESH,
                )
                all_of.wait_send()
                all_of.wait_recv()
            beam = pltpu.make_async_copy(recv.at[q, :, 0:16], beam_hbm.at[q], out_sem.at[1 + q])
            beam.start()
            copies.append(beam)

        @pl.loop(0, n)
        def _(src):
            block = jnp.concatenate([recv[g, src, 16:80, :], recv[2 + g, src, 16:80, :]], axis=0)
            block = block.astype(F32)
            by_part = block.reshape(8, 2, 8, 128)
            swapped = jnp.stack([by_part[:, 1], -by_part[:, 0]], axis=1).reshape(128, 128)
            for x, dest in ((block, plain), (swapped, turned)):
                t = x.T.astype(BF16)
                for f in range(HALF):
                    dest[src, g, :, f * 128 : f * 128 + 128] = t[f * SIG : f * SIG + SIG]

        for i, (mem, out) in enumerate(((plain, plain_hbm), (turned, turned_hbm))):
            copy = pltpu.make_async_copy(mem.at[:, g], out.at[:, g], out_sem.at[5 + 2 * g + i])
            copy.start()
            copies.append(copy)
    for copy in copies:
        copy.wait()


def exchange(volts, prototype, chan, delays, gains, mine, filled):
    vmem = pl.BlockSpec(memory_space=pltpu.VMEM)
    smem = pl.BlockSpec(memory_space=pltpu.SMEM)
    hbm = pl.BlockSpec(memory_space=pl.ANY)
    blocks = (4, GROUPS, ROWS, 128)
    spectra = (GROUPS, 2, SIG, 1024)
    weight = (PER_DEV, 2) + delays.shape
    return pl.pallas_call(
        exchange_kernel,
        out_shape=[
            jax.ShapeDtypeStruct(spectra, BF16),
            jax.ShapeDtypeStruct(spectra, BF16),
            jax.ShapeDtypeStruct((4, GROUPS, 16, 128), BF16),
            jax.ShapeDtypeStruct(weight, BF16),
        ],
        in_specs=[hbm, vmem, vmem, vmem, vmem, smem, smem],
        out_specs=[hbm] * 4,
        scratch_shapes=[
            pltpu.VMEM((2, 2, SIG, volts.shape[2]), BF16),
            pltpu.VMEM((5, 512, QUARTER), BF16),
            pltpu.VMEM((8, HALF, SIG, 128), F32),
            pltpu.VMEM((4, 256, QUARTER), BF16),
            pltpu.VMEM(blocks, BF16),
            pltpu.VMEM(blocks, BF16),
            pltpu.VMEM(spectra, BF16),
            pltpu.VMEM(spectra, BF16),
            pltpu.VMEM(weight, BF16),
            pltpu.SemaphoreType.DMA((2,)),
            pltpu.SemaphoreType.DMA((4,)),
            pltpu.SemaphoreType.DMA((4, len(PIECES))),
            pltpu.SemaphoreType.DMA((4, len(PIECES))),
            pltpu.SemaphoreType.DMA((9,)),
        ],
        compiler_params=pltpu.CompilerParams(
            vmem_limit_bytes=VMEM_LIMIT, collective_id=0, has_side_effects=True
        ),
        name="exchange",
    )(volts, prototype, chan, delays, gains, mine, filled)


def correlate_kernel(plain_ref, turned_ref, beam_ref, weight_ref, station_ref, vis_ref, beam_out_ref, wide):
    @pl.when(pl.program_id(0) == 0)
    def _():
        listed = station_ref.shape[1]
        row = lax.broadcasted_iota(jnp.int32, (512, listed), 0)
        station = (row & 31) * 16 + ((row >> 5) & 1) * 8 + (row >> 6)
        select = (station == station_ref[...]).astype(F32).astype(BF16)
        wide[...] = beam_ref[...].reshape(4 * 512, 128).astype(F32)
        rows = []
        for slot in range(PER_DEV):
            for part in range(2):
                for half in range(2):
                    first = half * 1024 + part * 8 + slot
                    x = wide[pl.ds(first, 64, stride=16), :]
                    t = x.T.astype(BF16)
                    rows.append(jnp.concatenate([t[s * 16 : s * 16 + 16] for s in range(8)], axis=1))
        picked = jnp.dot(jnp.concatenate(rows, axis=0), select, preferred_element_type=F32).astype(BF16)
        for slot in range(PER_DEV):
            pair = picked[slot * 64 : slot * 64 + 64]
            with_re = lax.dot_general(pair, weight_ref[slot, 0], NT, preferred_element_type=F32)
            with_im = lax.dot_general(pair, weight_ref[slot, 1], NT, preferred_element_type=F32)
            out_re = with_re[:32] - with_im[32:]
            out_im = with_re[32:] + with_im[:32]
            for part, out in enumerate((out_re, out_im)):
                for half in range(2):
                    for p in range(2):
                        at = half * 16 + p * 8
                        lanes = slice(p * 256, p * 256 + 256)
                        beam_out_ref[0, slot, part, half * 8 : half * 8 + 8, lanes] = out[at : at + 8]

    cols = pl.ds(pl.multiple_of(pl.program_id(0) * 256, 256), 256)
    scale = 1.0 / 512
    for part, left in enumerate((plain_ref, turned_ref)):
        total = lax.dot_general(left[...], plain_ref[cols, :], NT, preferred_element_type=F32)
        vis_ref[part, 0, 0] = total * scale


def correlate(plain, turned, beam, weight, station_index):
    once = pl.Buffered(1)

    def whole(x):
        zeros = (0,) * len(x.shape)
        return pl.BlockSpec(x.shape, lambda i: zeros, pipeline_mode=once)

    beam_out = jax.ShapeDtypeStruct((1, PER_DEV, 2, FRAMES, 512), F32)
    operands = (plain, turned, beam, weight, station_index)
    return pl.pallas_call(
        correlate_kernel,
        grid=(4,),
        out_shape=[jax.ShapeDtypeStruct((2, 1, 1, SIGNALS, SIGNALS), F32), beam_out],
        in_specs=[whole(x) for x in operands],
        out_specs=[
            pl.BlockSpec((2, 1, 1, SIGNALS, 256), lambda i: (0, 0, 0, 0, i)),
            whole(beam_out),
        ],
        scratch_shapes=[pltpu.VMEM((2048, 128), F32)],
        compiler_params=pltpu.CompilerParams(vmem_limit_bytes=VMEM_LIMIT),
        name="correlate",
    )(*operands)


def body(volts, prototype, beam_channels, station_index, delays, gains, assign):
    sb_here = lax.axis_index("sb")
    st_here = lax.axis_index("st")
    owners = assign[:, 0]
    order = jnp.arange(owners.shape[0], dtype=jnp.int32)
    matches = (owners == sb_here).astype(jnp.int32)
    position = jnp.sum((order[None, :] < order[:, None]).astype(jnp.int32) * matches[None, :], axis=1)
    row = jnp.arange(256, dtype=jnp.int32)
    slot = jnp.where((row & 7) < PER_DEV, (row >> 3) * PER_DEV + (row & 7), -1)
    picker = matches[None, :] * (position[None, :] == slot[:, None]).astype(jnp.int32)
    filled = jnp.sum(picker, axis=1)
    slot_channel = jnp.sum(picker * beam_channels[None, :], axis=1)
    line = jnp.arange(1024, dtype=jnp.int32)
    main = sb_here * BAND + (line & 255) * 4 + (line >> 8)
    mine = lax.dynamic_slice_in_dim(slot_channel, st_here * 8, 8)[None]
    there = lax.dynamic_slice_in_dim(filled, st_here * 8, 8)[None]
    chan = jnp.concatenate([main, slot_channel])[:, None]
    plain, turned, beam, weight = exchange(volts, prototype, chan, delays, gains, mine, there)
    rows = (SIGNALS, 1024)
    return tuple(correlate(plain.reshape(rows), turned.reshape(rows), beam, weight, station_index[None]))


def solution(mesh):
    in_specs = (P(None, "st", None), P(), P(), P(), P(), P(), P())
    out_specs = (P(None, "sb", "st", None, None), P("sb", "st", None, None, None))
    return jax.shard_map(body, mesh=mesh, in_specs=in_specs, out_specs=out_specs, check_vma=False)
```

time: 85.6 us -> 76.4 us (0.89)
  Pallas kernels: 79.2 us -> 72.1 us
  local copies, waits for them, and re-layouts: 3.66 us -> 1.68 us
    pallas_call x3 -> x2, Pallas kernels: 79.2 us -> 72.1 us  [the longest x1 61.7 us: exchange(): pl.pallas_call(exchange_kernel, out_shape=[jax.ShapeDtypeStruct(spectra,...]
    reshape x1 -> x0, local copies, waits for them, and re-layouts: 1.09 us -> none  [body(): x = recv[:, :, 0:16].reshape(2, 32, 2, 8, 256)[:, :, :, :PER_DEV]]
where the time goes in v3:
time: 76.4 us; the launch traced here: 76.2 us
  Pallas kernels  72.1 us (94%)
  other arithmetic  1.78 us (2%)
  local copies, waits for them, and re-layouts  1.68 us (2%)
    pallas_call x1, Pallas kernels, exchange(): pl.pallas_call(exchange_kernel, out_shape=[jax.ShapeDtypeStruct(spectra,...  61.7 us
    pallas_call x1, Pallas kernels, correlate(): pl.pallas_call(correlate_kernel, grid=(4,), out_shape=[jax.ShapeDtypeStru...  10.4 us

profile of v3, /device:TPU:1, one launch (start us, length us, event | category | flops | bytes accessed | tf_op | source)
XLA Modules:
  0.0 76.2 jit_solution(3255662883111151117)
XLA Ops:
  0.6 0.7 fusion.1
  1.3 0.1 select_reduce_fusion
  1.5 0.9 %select_reduce_fusion.1 = (s32[256]{0:T(256)S(1)}, s32[256]{0:T(256)S(1)}) fusion(s32[384]{0:T(512)S(1)} %fusion.1, s32[384]{0:T(512)S(1)} %select_reduce_fusion, s32[256]{0:T(256)S(1)} %compare_select_fusion, s32[384]{0:T(512)} %param.9), kind=kLoop, calls=%fused_computation.2 | loop fusion | flops 491008 | bytes 7680 | tf_op jit(solution)/shard_map/reduce_sum | solution.py:356
  2.4 0.6 dynamic-slice_bitcast_fusion
  3.0 1.1 %broadcast_in_dim.28.chan_ref = s32[1280,1]{1,0:T(8,128)} reshape(s32[1280]{0:T(1024)S(1)} %pad_add_fusion) | data formatting | bytes 10240 | tf_op jit(solution)/shard_map/broadcast_in_dim | solution.py:362
  4.1 61.7 %exchange.1 = (bf16[32,2,16,1024]{3,2,1,0:T(8,128)(2,1)}, bf16[32,2,16,1024]{3,2,1,0:T(8,128)(2,1)}, bf16[4,32,16,128]{3,2,1,0:T(8,128)(2,1)}, bf16[5,2,256,256]{3,2,1,0:T(8,128)(2,1)}) custom-call(bf16[2,32,126976]{2,1,0:T(8,128)(2,1)} %volts_hbm.1, f32[16,4096]{1,0:T(8,128)} %proto_ref.1, s32[1280,1]{1,0:T(8,128)} %broadcast_in_dim.28.chan_ref, ...), custom_call_target="tpu_custom_call" | custom-call | tf_op jit(solution)/shard_map/exchange/pallas_call | solution.py:252
  65.8 10.4 %correlate.1 = (f32[2,1,1,1024,1024]{4,3,2,1,0:T(8,128)}, f32[1,5,2,16,512]{4,3,2,1,0:T(8,128)}) custom-call(bf16[1024,1024]{1,0:T(8,128)(2,1)} %bitcast.7, bf16[1024,1024]{1,0:T(8,128)(2,1)} %bitcast.8, bf16[4,32,16,128]{3,2,1,0:T(8,128)(2,1)} %get-tuple-element.8.beam_ref, bf16[5,2,256,256]{3,2,1,0:T(8,128)(2,1)} %get-tuple-element.9.weight_ref, ...), custom_call_target="tpu_custom_call" | custom-call | tf_op jit(solution)/shard_map/correlate/pallas_call | solution.py:331
  (3 shorter events, 0.0 us)

commit v4 on v3

--- a/solution.py
+++ b/solution.py
@@ -44,23 +44,49 @@
     return s, c
 
 
-def fill_tables(chan_ref, table):
-    @pl.loop(0, chan_ref.shape[0] // 32)
-    def _(block):
-        at = pl.ds(pl.multiple_of(block * 32, 32), 32)
-        wide = jnp.broadcast_to(chan_ref[at, :], (32, 128))
+def fill_slots(owner_ref, channel_ref, slots):
+    entries = owner_ref.shape[1]
+    match = owner_ref[...] == lax.axis_index("sb")
+    ones = jnp.broadcast_to(match.astype(F32), (8, entries)).astype(BF16)
+    row = lax.broadcasted_iota(jnp.int32, (entries, entries), 0)
+    col = lax.broadcasted_iota(jnp.int32, (entries, entries), 1)
+    earlier = (row < col).astype(F32).astype(BF16)
+    position = jnp.dot(ones, earlier, preferred_element_type=F32)[0:1].astype(jnp.int32)
+    position = jnp.where(match, position, -1)
+    line = lax.broadcasted_iota(jnp.int32, (SLOTS, entries), 0)
+    pick = (position == (line & 31) * PER_DEV + (line >> 5)).astype(F32)
+    chan = jnp.sum(pick * channel_ref[...].astype(F32), axis=1, keepdims=True)
+    filled = jnp.sum(pick, axis=1, keepdims=True)
+    slots[0] = jnp.broadcast_to(chan, (SLOTS, 256))
+    slots[1] = jnp.broadcast_to(filled, (SLOTS, 256))
+
+
+def fill_tables(slots, table):
+    def fill(wide, which, cos_row, sin_row):
         lane = lax.broadcasted_iota(jnp.int32, (32, 128), 1)
         s, c = sincos_turns(((lane * wide) & (NCH - 1)).astype(F32) * (1.0 / NCH))
         s_step, c_step = sincos_turns(((128 * wide) & (NCH - 1)).astype(F32) * (1.0 / NCH))
         s, c = s * (1.0 / 64), c * (1.0 / 64)
-        which = block // 8
-        cos_at = pl.ds(pl.multiple_of((block % 8) * 32, 32), 32)
-        sin_at = pl.ds(pl.multiple_of((block % 8) * 32 + 256, 32), 32)
+        cos_at = pl.ds(pl.multiple_of(cos_row, 32), 32)
+        sin_at = pl.ds(pl.multiple_of(sin_row, 32), 32)
         for tile in range(QUARTER // 128):
             lanes = slice(tile * 128, tile * 128 + 128)
             table[which, cos_at, lanes] = c.astype(BF16)
             table[which, sin_at, lanes] = s.astype(BF16)
             s, c = s * c_step + c * s_step, c * c_step - s * s_step
+
+    first = lax.axis_index("sb") * BAND
+
+    @pl.loop(0, 32)
+    def _(block):
+        k1, row = block // 8, (block % 8) * 32
+        line = lax.broadcasted_iota(jnp.int32, (32, 128), 0)
+        fill(first + (row + line) * 4 + k1, k1, row, row + 256)
+
+    @pl.loop(0, SLOTS // 32)
+    def _(block):
+        rows = pl.ds(pl.multiple_of(block * 32, 32), 32)
+        fill(slots[0, rows, 0:128].astype(jnp.int32), 4, block * 32, block * 32 + SLOTS)
 
 
 def filter_frames(volts, half, proto_ref, filt, spec):
@@ -73,18 +99,28 @@
                 jnp.broadcast_to(proto_ref[t : t + 1, pl.ds(base, 128)], (SIG, 128))
                 for t in range(TAPS)
             ]
+            h0, h1 = taps[0::2], taps[1::2]
+            hd = [b - a for a, b in zip(h0, h1)]
             for part in range(2):
-                acc = [None] * HALF
-                for u in range(HALF + TAPS - 1):
+
+                def frame(u):
                     at = pl.multiple_of((half * HALF + u) * NCH + base, 128)
-                    v = volts[part, :, pl.ds(at, 128)].astype(F32)
-                    for f in range(HALF):
-                        t = u - f
-                        if 0 <= t < TAPS:
-                            term = taps[t] * v
-                            acc[f] = term if acc[f] is None else acc[f] + term
-                for f in range(HALF):
-                    filt[part * 4 + n1, f] = acc[f]
+                    return volts[part, :, pl.ds(at, 128)].astype(F32)
+
+                acc = [[None] * (HALF // 2) for _ in range(3)]
+                x0 = frame(0)
+                for j in range((HALF + TAPS) // 2 - 1):
+                    x1, after = frame(2 * j + 1), frame(2 * j + 2)
+                    terms = ((hd, x1), (h0, x0 + x1), (h1, x1 + after))
+                    for m in range(HALF // 2):
+                        i = j - m
+                        if 0 <= i < TAPS // 2:
+                            for total, (h, x) in zip(acc, terms):
+                                total[m] = h[i] * x if total[m] is None else total[m] + h[i] * x
+                    x0 = after
+                for m in range(HALF // 2):
+                    filt[part * 4 + n1, 2 * m] = acc[1][m] + acc[0][m]
+                    filt[part * 4 + n1, 2 * m + 1] = acc[2][m] - acc[0][m]
 
         lanes = pl.ds(pl.multiple_of(tile * 128, 128), 128)
         for f in range(HALF):
@@ -107,9 +143,9 @@
 
 
 def exchange_kernel(
-    volts_hbm, proto_ref, chan_ref, delay_ref, gain_ref, mine_ref, filled_ref,
+    volts_hbm, proto_ref, owner_ref, channel_ref, delay_ref, gain_ref,
     plain_hbm, turned_hbm, beam_hbm, weight_hbm,
-    volts, table, filt, spec, send, recv, plain, turned, weight,
+    volts, slots, place, table, filt, spec, send, recv, plain, turned, weight,
     load_sem, own_sem, send_sem, recv_sem, out_sem,
 ):
     n = GROUPS
@@ -127,7 +163,12 @@
         there = lax.rem(me + d, n)
         pl.semaphore_signal(barrier, inc=1, device_id={"st": there}, device_id_type=MESH)
 
-    fill_tables(chan_ref, table)
+    fill_slots(owner_ref, channel_ref, slots)
+    fill_tables(slots, table)
+    row = lax.broadcasted_iota(jnp.int32, (512, 2 * SLOTS), 0)
+    col = lax.broadcasted_iota(jnp.int32, (512, 2 * SLOTS), 1)
+    taken = ((row >> 3) & 1) * SLOTS + (row & 7) * 32 + (row >> 4)
+    place[...] = ((taken == col) & ((row & 7) < PER_DEV)).astype(F32).astype(BF16)
     load(1).start()
     pl.semaphore_wait(barrier, n - 1)
 
@@ -163,27 +204,28 @@
 
         filter_frames(volts.at[g], half, proto_ref, filt, spec)
 
-        def both(k1, which):
-            t = lax.dot_general(table[which], spec[k1], NT, preferred_element_type=F32)
-            c, s = t[:256], t[256:]
+        def both(k1, which, rows):
+            t = lax.dot_general(table[which, : 2 * rows], spec[k1], NT, preferred_element_type=F32)
+            c, s = t[:rows], t[rows:]
             return c[:, :128] + s[:, 128:], c[:, 128:] - s[:, :128]
 
-        chan = chan_ref[1024:1280, :]
-        beam_re = jnp.zeros((256, 128), F32)
-        beam_im = jnp.zeros((256, 128), F32)
+        chan = slots[0, :, 0:128].astype(jnp.int32)
+        beam_re = jnp.zeros((SLOTS, 128), F32)
+        beam_im = jnp.zeros((SLOTS, 128), F32)
         for k1 in range(4):
-            re, im = both(k1, 4)
+            re, im = both(k1, 4, SLOTS)
             mine = (chan & 3) == k1
             beam_re = jnp.where(mine, re, beam_re)
             beam_im = jnp.where(mine, im, beam_im)
         row = lax.broadcasted_iota(jnp.int32, (128, 128), 0)
         col = lax.broadcasted_iota(jnp.int32, (128, 128), 1)
         turn = (row == (col & 7) * 16 + (col >> 3)).astype(F32).astype(BF16)
-        joined = by_group(beam_re, beam_im).reshape(512, 128)
-        placed = jnp.dot(joined, turn, preferred_element_type=F32)
+        joined = jnp.concatenate([beam_re, beam_im], axis=0).astype(BF16)
+        joined = jnp.dot(joined, turn, preferred_element_type=F32).astype(BF16)
+        placed = jnp.dot(place[...], joined, preferred_element_type=F32)
         send[q, :, 0:16, :] = placed.astype(BF16).reshape(32, 16, 128)
         for k1 in range(4):
-            re, im = both(k1, k1)
+            re, im = both(k1, k1, 256)
             send[q, :, 16 + k1 * 16 : 32 + k1 * 16, :] = by_group(re, im)
             if k1 % 2 == 1:
                 start(q, k1 // 2)
@@ -194,10 +236,11 @@
         at = pl.ds(pl.multiple_of(block * 32, 32), 32)
         scaling = gain_ref[at, :] * (1.0 / math.sqrt(gain_ref.shape[1]))
         for slot in range(PER_DEV):
-            turns = delay_ref[at, :] * (mine_ref[0, slot].astype(F32) * (1.0 / NCH))
+            mine = pl.ds(slot * 32 + me, 1)
+            turns = delay_ref[at, :] * (slots[0, mine, :] * (1.0 / NCH))
             turns = turns - jnp.floor(turns)
             s, c = sincos_turns(turns)
-            level = scaling * filled_ref[0, slot].astype(F32)
+            level = scaling * slots[1, mine, :]
             weight[slot, 0, at, :] = (level * c).astype(BF16)
             weight[slot, 1, at, :] = (-level * s).astype(BF16)
 
@@ -242,9 +285,8 @@
         copy.wait()
 
 
-def exchange(volts, prototype, chan, delays, gains, mine, filled):
+def exchange(volts, prototype, owners, channels, delays, gains):
     vmem = pl.BlockSpec(memory_space=pltpu.VMEM)
-    smem = pl.BlockSpec(memory_space=pltpu.SMEM)
     hbm = pl.BlockSpec(memory_space=pl.ANY)
     blocks = (4, GROUPS, ROWS, 128)
     spectra = (GROUPS, 2, SIG, 1024)
@@ -257,10 +299,12 @@
             jax.ShapeDtypeStruct((4, GROUPS, 16, 128), BF16),
             jax.ShapeDtypeStruct(weight, BF16),
         ],
-        in_specs=[hbm, vmem, vmem, vmem, vmem, smem, smem],
+        in_specs=[hbm] + [vmem] * 5,
         out_specs=[hbm] * 4,
         scratch_shapes=[
             pltpu.VMEM((2, 2, SIG, volts.shape[2]), BF16),
+            pltpu.VMEM((2, SLOTS, 256), F32),
+            pltpu.VMEM((512, 2 * SLOTS), BF16),
             pltpu.VMEM((5, 512, QUARTER), BF16),
             pltpu.VMEM((8, HALF, SIG, 128), F32),
             pltpu.VMEM((4, 256, QUARTER), BF16),
@@ -279,7 +323,7 @@
             vmem_limit_bytes=VMEM_LIMIT, collective_id=0, has_side_effects=True
         ),
         name="exchange",
-    )(volts, prototype, chan, delays, gains, mine, filled)
+    )(volts, prototype, owners, channels, delays, gains)
 
 
 def correlate_kernel(plain_ref, turned_ref, beam_ref, weight_ref, station_ref, vis_ref, beam_out_ref, wide):
@@ -344,23 +388,8 @@
 
 
 def body(volts, prototype, beam_channels, station_index, delays, gains, assign):
-    sb_here = lax.axis_index("sb")
-    st_here = lax.axis_index("st")
-    owners = assign[:, 0]
-    order = jnp.arange(owners.shape[0], dtype=jnp.int32)
-    matches = (owners == sb_here).astype(jnp.int32)
-    position = jnp.sum((order[None, :] < order[:, None]).astype(jnp.int32) * matches[None, :], axis=1)
-    row = jnp.arange(256, dtype=jnp.int32)
-    slot = jnp.where((row & 7) < PER_DEV, (row >> 3) * PER_DEV + (row & 7), -1)
-    picker = matches[None, :] * (position[None, :] == slot[:, None]).astype(jnp.int32)
-    filled = jnp.sum(picker, axis=1)
-    slot_channel = jnp.sum(picker * beam_channels[None, :], axis=1)
-    line = jnp.arange(1024, dtype=jnp.int32)
-    main = sb_here * BAND + (line & 255) * 4 + (line >> 8)
-    mine = lax.dynamic_slice_in_dim(slot_channel, st_here * 8, 8)[None]
-    there = lax.dynamic_slice_in_dim(filled, st_here * 8, 8)[None]
-    chan = jnp.concatenate([main, slot_channel])[:, None]
-    plain, turned, beam, weight = exchange(volts, prototype, chan, delays, gains, mine, there)
+    owners = assign.reshape(1, -1)
+    plain, turned, beam, weight = exchange(volts, prototype, owners, beam_channels[None], delays, gains)
     rows = (SIGNALS, 1024)
     return tuple(correlate(plain.reshape(rows), turned.reshape(rows), beam, weight, station_index[None]))
 

time: 76.4 us -> 68.9 us (0.902)
  Pallas kernels: 72.1 us -> 66.8 us
  other arithmetic: 1.78 us -> 0 us
    pallas_call x1, Pallas kernels: 61.7 us -> 56.4 us  [exchange(): pl.pallas_call(exchange_kernel, out_shape=[jax.ShapeDtypeStruct(spectra,...]
    reduce_sum x2 -> x0, other arithmetic: 1.06 us -> none  [the longest x1 0.91 us: body(): filled = jnp.sum(picker, axis=1)]
    broadcast_in_dim x2 -> x1, local copies, waits for them, and re-layouts: 1.68 us -> 1.25 us  [body(): beam_channels[None]]
where the time goes in v4:
time: 68.9 us; the launch traced here: 68.7 us
  Pallas kernels  66.8 us (97%)
  local copies, waits for them, and re-layouts  1.25 us (2%)
    pallas_call x1, Pallas kernels, exchange(): pl.pallas_call(exchange_kernel, out_shape=[jax.ShapeDtypeStruct(spectra,...  56.4 us
    pallas_call x1, Pallas kernels, correlate(): pl.pallas_call(correlate_kernel, grid=(4,), out_shape=[jax.ShapeDtypeStru...  10.4 us

profile of v4, /device:TPU:1, one launch (start us, length us, event | category | flops | bytes accessed | tf_op | source)
XLA Modules:
  0.0 68.7 jit_solution(14990612764035675001)
XLA Ops:
  0.6 1.2 %broadcast_in_dim.6.channel_ref = s32[1,384]{1,0:T(1,128)} reshape(s32[384]{0:T(512)} %param.9) | data formatting | bytes 3072 | tf_op jit(solution)/shard_map/broadcast_in_dim | solution.py:392
  1.9 56.4 %exchange.1 = (bf16[32,2,16,1024]{3,2,1,0:T(8,128)(2,1)}, bf16[32,2,16,1024]{3,2,1,0:T(8,128)(2,1)}, bf16[4,32,16,128]{3,2,1,0:T(8,128)(2,1)}, bf16[5,2,256,256]{3,2,1,0:T(8,128)(2,1)}) custom-call(bf16[2,32,126976]{2,1,0:T(8,128)(2,1)} %volts_hbm.1, f32[16,4096]{1,0:T(8,128)} %proto_ref.1, s32[1,384]{1,0:T(1,128)} %bitcast.6, ...), custom_call_target="tpu_custom_call" | custom-call | tf_op jit(solution)/shard_map/exchange/pallas_call | solution.py:294
  58.3 10.4 %correlate.1 = (f32[2,1,1,1024,1024]{4,3,2,1,0:T(8,128)}, f32[1,5,2,16,512]{4,3,2,1,0:T(8,128)}) custom-call(bf16[1024,1024]{1,0:T(8,128)(2,1)} %bitcast.4, bf16[1024,1024]{1,0:T(8,128)(2,1)} %bitcast.5, bf16[4,32,16,128]{3,2,1,0:T(8,128)(2,1)} %get-tuple-element.8.beam_ref, bf16[5,2,256,256]{3,2,1,0:T(8,128)(2,1)} %get-tuple-element.9.weight_ref, ...), custom_call_target="tpu_custom_call" | custom-call | tf_op jit(solution)/shard_map/correlate/pallas_call | solution.py:375

commit v5 on v4

--- a/solution.py
+++ b/solution.py
@@ -55,7 +55,7 @@
     position = jnp.where(match, position, -1)
     line = lax.broadcasted_iota(jnp.int32, (SLOTS, entries), 0)
     pick = (position == (line & 31) * PER_DEV + (line >> 5)).astype(F32)
-    chan = jnp.sum(pick * channel_ref[...].astype(F32), axis=1, keepdims=True)
+    chan = jnp.sum(pick * channel_ref[...].reshape(1, entries).astype(F32), axis=1, keepdims=True)
     filled = jnp.sum(pick, axis=1, keepdims=True)
     slots[0] = jnp.broadcast_to(chan, (SLOTS, 256))
     slots[1] = jnp.broadcast_to(filled, (SLOTS, 256))
@@ -273,7 +273,7 @@
             by_part = block.reshape(8, 2, 8, 128)
             swapped = jnp.stack([by_part[:, 1], -by_part[:, 0]], axis=1).reshape(128, 128)
             for x, dest in ((block, plain), (swapped, turned)):
-                t = x.T.astype(BF16)
+                t = x.astype(BF16).T
                 for f in range(HALF):
                     dest[src, g, :, f * 128 : f * 128 + 128] = t[f * SIG : f * SIG + SIG]
 
@@ -389,7 +389,7 @@
 
 def body(volts, prototype, beam_channels, station_index, delays, gains, assign):
     owners = assign.reshape(1, -1)
-    plain, turned, beam, weight = exchange(volts, prototype, owners, beam_channels[None], delays, gains)
+    plain, turned, beam, weight = exchange(volts, prototype, owners, beam_channels, delays, gains)
     rows = (SIGNALS, 1024)
     return tuple(correlate(plain.reshape(rows), turned.reshape(rows), beam, weight, station_index[None]))
 

time: 68.9 us -> 66.8 us (0.970)
  local copies, waits for them, and re-layouts: 1.25 us -> 0 us
  Pallas kernels: 66.8 us -> 66 us
    broadcast_in_dim x1 -> x0, local copies, waits for them, and re-layouts: 1.25 us -> none  [body(): beam_channels[None]]
    pallas_call x1, Pallas kernels: 56.4 us -> 55.6 us  [exchange(): pl.pallas_call(exchange_kernel, out_shape=[jax.ShapeDtypeStruct(spectra,...]
where the time goes in v5:
time: 66.8 us; the launch traced here: 66.6 us
  Pallas kernels  66 us (99%)
    pallas_call x1, Pallas kernels, exchange(): pl.pallas_call(exchange_kernel, out_shape=[jax.ShapeDtypeStruct(spectra,...  55.6 us
    pallas_call x1, Pallas kernels, correlate(): pl.pallas_call(correlate_kernel, grid=(4,), out_shape=[jax.ShapeDtypeStru...  10.4 us

profile of v5, /device:TPU:1, one launch (start us, length us, event | category | flops | bytes accessed | tf_op | source)
XLA Modules:
  0.0 66.6 jit_solution(6287216996201322354)
XLA Ops:
  0.6 55.6 %exchange.1 = (bf16[32,2,16,1024]{3,2,1,0:T(8,128)(2,1)}, bf16[32,2,16,1024]{3,2,1,0:T(8,128)(2,1)}, bf16[4,32,16,128]{3,2,1,0:T(8,128)(2,1)}, bf16[5,2,256,256]{3,2,1,0:T(8,128)(2,1)}) custom-call(bf16[2,32,126976]{2,1,0:T(8,128)(2,1)} %volts_hbm.1, f32[16,4096]{1,0:T(8,128)} %proto_ref.1, s32[1,384]{1,0:T(1,128)} %bitcast.6, s32[384]{0:T(512)} %channel_ref.1, ...), custom_call_target="tpu_custom_call" | custom-call | tf_op jit(solution)/shard_map/exchange/pallas_call | solution.py:294
  56.2 10.4 %correlate.1 = (f32[2,1,1,1024,1024]{4,3,2,1,0:T(8,128)}, f32[1,5,2,16,512]{4,3,2,1,0:T(8,128)}) custom-call(bf16[1024,1024]{1,0:T(8,128)(2,1)} %bitcast.4, bf16[1024,1024]{1,0:T(8,128)(2,1)} %bitcast.5, bf16[4,32,16,128]{3,2,1,0:T(8,128)(2,1)} %get-tuple-element.8.beam_ref, bf16[5,2,256,256]{3,2,1,0:T(8,128)(2,1)} %get-tuple-element.9.weight_ref, ...), custom_call_target="tpu_custom_call" | custom-call | tf_op jit(solution)/shard_map/correlate/pallas_call | solution.py:375

commit v6 on v5

--- a/solution.py
+++ b/solution.py
@@ -96,31 +96,32 @@
         def _(n1):
             base = pl.multiple_of(n1 * QUARTER + tile * 128, 128)
             taps = [
-                jnp.broadcast_to(proto_ref[t : t + 1, pl.ds(base, 128)], (SIG, 128))
+                jnp.broadcast_to(proto_ref[t : t + 1, pl.ds(base, 128)], (8, 128))
                 for t in range(TAPS)
             ]
             h0, h1 = taps[0::2], taps[1::2]
             hd = [b - a for a, b in zip(h0, h1)]
             for part in range(2):
-
-                def frame(u):
-                    at = pl.multiple_of((half * HALF + u) * NCH + base, 128)
-                    return volts[part, :, pl.ds(at, 128)].astype(F32)
-
-                acc = [[None] * (HALF // 2) for _ in range(3)]
-                x0 = frame(0)
-                for j in range((HALF + TAPS) // 2 - 1):
-                    x1, after = frame(2 * j + 1), frame(2 * j + 2)
-                    terms = ((hd, x1), (h0, x0 + x1), (h1, x1 + after))
+                for rows in (slice(0, 8), slice(8, 16)):
+
+                    def frame(u):
+                        at = pl.multiple_of((half * HALF + u) * NCH + base, 128)
+                        return volts[part, rows, pl.ds(at, 128)].astype(F32)
+
+                    acc = [[None] * (HALF // 2) for _ in range(3)]
+                    x0 = frame(0)
+                    for j in range((HALF + TAPS) // 2 - 1):
+                        x1, after = frame(2 * j + 1), frame(2 * j + 2)
+                        terms = ((hd, x1), (h0, x0 + x1), (h1, x1 + after))
+                        for m in range(HALF // 2):
+                            i = j - m
+                            if 0 <= i < TAPS // 2:
+                                for total, (h, x) in zip(acc, terms):
+                                    total[m] = h[i] * x if total[m] is None else total[m] + h[i] * x
+                        x0 = after
                     for m in range(HALF // 2):
-                        i = j - m
-                        if 0 <= i < TAPS // 2:
-                            for total, (h, x) in zip(acc, terms):
-                                total[m] = h[i] * x if total[m] is None else total[m] + h[i] * x
-                    x0 = after
-                for m in range(HALF // 2):
-                    filt[part * 4 + n1, 2 * m] = acc[1][m] + acc[0][m]
-                    filt[part * 4 + n1, 2 * m + 1] = acc[2][m] - acc[0][m]
+                        filt[part * 4 + n1, 2 * m, rows] = acc[1][m] + acc[0][m]
+                        filt[part * 4 + n1, 2 * m + 1, rows] = acc[2][m] - acc[0][m]
 
         lanes = pl.ds(pl.multiple_of(tile * 128, 128), 128)
         for f in range(HALF):

time: 66.8 us -> 66.3 us (level)
  no operation moved by 1% of the time
where the time goes in v6:
time: 66.3 us; the launch traced here: 66.2 us
  Pallas kernels  65.6 us (99%)
    pallas_call x1, Pallas kernels, exchange(): pl.pallas_call(exchange_kernel, out_shape=[jax.ShapeDtypeStruct(spectra,...  55.2 us
    pallas_call x1, Pallas kernels, correlate(): pl.pallas_call(correlate_kernel, grid=(4,), out_shape=[jax.ShapeDtypeStru...  10.4 us

profile of v6, /device:TPU:1, one launch (start us, length us, event | category | flops | bytes accessed | tf_op | source)
XLA Modules:
  0.0 66.2 jit_solution(4899910345033030424)
XLA Ops:
  0.6 55.2 %exchange.1 = (bf16[32,2,16,1024]{3,2,1,0:T(8,128)(2,1)}, bf16[32,2,16,1024]{3,2,1,0:T(8,128)(2,1)}, bf16[4,32,16,128]{3,2,1,0:T(8,128)(2,1)}, bf16[5,2,256,256]{3,2,1,0:T(8,128)(2,1)}) custom-call(bf16[2,32,126976]{2,1,0:T(8,128)(2,1)} %volts_hbm.1, f32[16,4096]{1,0:T(8,128)} %proto_ref.1, s32[1,384]{1,0:T(1,128)} %bitcast.6, s32[384]{0:T(512)} %channel_ref.1, ...), custom_call_target="tpu_custom_call" | custom-call | tf_op jit(solution)/shard_map/exchange/pallas_call | solution.py:295
  55.8 10.4 %correlate.1 = (f32[2,1,1,1024,1024]{4,3,2,1,0:T(8,128)}, f32[1,5,2,16,512]{4,3,2,1,0:T(8,128)}) custom-call(bf16[1024,1024]{1,0:T(8,128)(2,1)} %bitcast.4, bf16[1024,1024]{1,0:T(8,128)(2,1)} %bitcast.5, bf16[4,32,16,128]{3,2,1,0:T(8,128)(2,1)} %get-tuple-element.8.beam_ref, bf16[5,2,256,256]{3,2,1,0:T(8,128)(2,1)} %get-tuple-element.9.weight_ref, ...), custom_call_target="tpu_custom_call" | custom-call | tf_op jit(solution)/shard_map/correlate/pallas_call | solution.py:376

commit v7 on v6

--- a/solution.py
+++ b/solution.py
@@ -23,7 +23,7 @@
 BF16 = jnp.bfloat16
 VMEM_LIMIT = 56 << 20
 MESH = pl.DeviceIdType.MESH
-PIECES = ((0, 48), (48, 32))
+PIECES = ((0, 32), (32, 48))
 HALF = 8
 CHIPS = ((2, 2), (1, 2), (2, 1), (3, 2), (2, 3), (0, 2), (2, 0), (1, 1), (3, 3), (1, 3), (3, 1), (0, 1), (3, 0), (0, 3), (1, 0))
 ORDER = tuple((z, x, c) for z, x in CHIPS for c in range(2)) + ((0, 0, 1),)
@@ -210,6 +210,11 @@
             c, s = t[:rows], t[rows:]
             return c[:, :128] + s[:, 128:], c[:, 128:] - s[:, :128]
 
+        for k1 in range(4):
+            re, im = both(k1, k1, 256)
+            send[q, :, k1 * 16 : k1 * 16 + 16, :] = by_group(re, im)
+            if k1 == 1:
+                start(q, 0)
         chan = slots[0, :, 0:128].astype(jnp.int32)
         beam_re = jnp.zeros((SLOTS, 128), F32)
         beam_im = jnp.zeros((SLOTS, 128), F32)
@@ -224,12 +229,8 @@
         joined = jnp.concatenate([beam_re, beam_im], axis=0).astype(BF16)
         joined = jnp.dot(joined, turn, preferred_element_type=F32).astype(BF16)
         placed = jnp.dot(place[...], joined, preferred_element_type=F32)
-        send[q, :, 0:16, :] = placed.astype(BF16).reshape(32, 16, 128)
-        for k1 in range(4):
-            re, im = both(k1, k1, 256)
-            send[q, :, 16 + k1 * 16 : 32 + k1 * 16, :] = by_group(re, im)
-            if k1 % 2 == 1:
-                start(q, k1 // 2)
+        send[q, :, 64:80, :] = placed.astype(BF16).reshape(32, 16, 128)
+        start(q, 1)
         own(q).start()
 
     @pl.loop(0, delay_ref.shape[0] // 32)
@@ -263,13 +264,13 @@
                 )
                 all_of.wait_send()
                 all_of.wait_recv()
-            beam = pltpu.make_async_copy(recv.at[q, :, 0:16], beam_hbm.at[q], out_sem.at[1 + q])
+            beam = pltpu.make_async_copy(recv.at[q, :, 64:80], beam_hbm.at[q], out_sem.at[1 + q])
             beam.start()
             copies.append(beam)
 
         @pl.loop(0, n)
         def _(src):
-            block = jnp.concatenate([recv[g, src, 16:80, :], recv[2 + g, src, 16:80, :]], axis=0)
+            block = jnp.concatenate([recv[g, src, 0:64, :], recv[2 + g, src, 0:64, :]], axis=0)
             block = block.astype(F32)
             by_part = block.reshape(8, 2, 8, 128)
             swapped = jnp.stack([by_part[:, 1], -by_part[:, 0]], axis=1).reshape(128, 128)

time: 66.3 us -> 65.1 us (0.982)
  Pallas kernels: 65.6 us -> 64.3 us
    pallas_call x1, Pallas kernels: 55.2 us -> 53.9 us  [exchange(): pl.pallas_call(exchange_kernel, out_shape=[jax.ShapeDtypeStruct(spectra,...]
where the time goes in v7:
time: 65.1 us; the launch traced here: 64.9 us
  Pallas kernels  64.3 us (99%)
    pallas_call x1, Pallas kernels, exchange(): pl.pallas_call(exchange_kernel, out_shape=[jax.ShapeDtypeStruct(spectra,...  53.9 us
    pallas_call x1, Pallas kernels, correlate(): pl.pallas_call(correlate_kernel, grid=(4,), out_shape=[jax.ShapeDtypeStru...  10.4 us

profile of v7, /device:TPU:1, one launch (start us, length us, event | category | flops | bytes accessed | tf_op | source)
XLA Modules:
  0.0 64.9 jit_solution(13116533601907966262)
XLA Ops:
  0.6 53.9 %exchange.1 = (bf16[32,2,16,1024]{3,2,1,0:T(8,128)(2,1)}, bf16[32,2,16,1024]{3,2,1,0:T(8,128)(2,1)}, bf16[4,32,16,128]{3,2,1,0:T(8,128)(2,1)}, bf16[5,2,256,256]{3,2,1,0:T(8,128)(2,1)}) custom-call(bf16[2,32,126976]{2,1,0:T(8,128)(2,1)} %volts_hbm.1, f32[16,4096]{1,0:T(8,128)} %proto_ref.1, s32[1,384]{1,0:T(1,128)} %bitcast.6, s32[384]{0:T(512)} %channel_ref.1, ...), custom_call_target="tpu_custom_call" | custom-call | tf_op jit(solution)/shard_map/exchange/pallas_call | solution.py:296
  54.5 10.4 %correlate.1 = (f32[2,1,1,1024,1024]{4,3,2,1,0:T(8,128)}, f32[1,5,2,16,512]{4,3,2,1,0:T(8,128)}) custom-call(bf16[1024,1024]{1,0:T(8,128)(2,1)} %bitcast.4, bf16[1024,1024]{1,0:T(8,128)(2,1)} %bitcast.5, bf16[4,32,16,128]{3,2,1,0:T(8,128)(2,1)} %get-tuple-element.8.beam_ref, bf16[5,2,256,256]{3,2,1,0:T(8,128)(2,1)} %get-tuple-element.9.weight_ref, ...), custom_call_target="tpu_custom_call" | custom-call | tf_op jit(solution)/shard_map/correlate/pallas_call | solution.py:377
